TPU v7x, 32 devices: a whole 2x2x4 slice. The times are simulated.
32 devices in a mesh: space: 4 (over x, core), tile: 8 (over z, y).
Axes of the slice: x: 2, y: 2, z: 4, core: 2. Of those that a mesh axis runs over, the one named last changes fastest.
Arguments:
- atom_feat: bfloat16 [512, 128, 128], P(('space', 'tile')), may hold values from -6 to 6
- atom_pos: bfloat16 [512, 3, 128], P(('space', 'tile')), may hold values from 0 to 4
- atom_counts: int32 [512], P(('space', 'tile')), may hold values from 32 to 128
- atom_nbrs: int32 [512, 4], P(('space', 'tile')), may hold values from 0 to 511, as said below
- probe_pos: float32 [64, 3, 512], P(('space', 'tile')), may hold values from 0 to 4
- probe_target: float32 [64, 512], P(('space', 'tile')), may hold values from -6 to 6
- tile_blocks: int32 [64, 8], P(('space', 'tile')), may hold values from 0 to 511, as said below
- atom_filter: bfloat16 [128, 1024], replicated, may hold values from -0.5 to 0.5
- probe_filter: bfloat16 [128, 1024], replicated, may hold values from -0.5 to 0.5
- mix_weight: bfloat16 [128, 128], replicated, may hold values from -0.5 to 0.5
- readout: float32 [128], replicated, may hold values from -0.5 to 0.5
Outputs:
- density: float32 [64, 512], P(('space', 'tile'))
- atom_filter_grad: float32 [128, 1024], replicated
- probe_filter_grad: float32 [128, 1024], replicated
- mix_grad: float32 [128, 128], replicated
- readout_grad: float32 [128], replicated
Inputs may be any that keep to these rules, and one draw needn't show every extreme that they name: `atom_nbrs`: block g lies on device g // 16 in the order space then tile. The 4 neighbours of a block lie on devices of the same tile index whose space index differs by at most one, cyclically: the first one lower, the second one higher, the third the same; they need not be distinct. `tile_blocks`: the 8 blocks of a tile are distinct and lie on devices of the tile's own space index. The tiles of one device read at most 4 distinct blocks from any one device, and exactly 4 from some device.
All inputs are finite; a program needn't handle non-finite values.
Results may differ from a plain program's by a relative error of at most 0.0061.
Values may be sent and summed in bfloat16 or wider, within the bound.
A program may use at most 64 MiB of HBM per device.

v0:
```python
import jax
import jax.numpy as jnp
from jax import lax
from jax.sharding import PartitionSpec as P

CUTOFF = 6.0
SPACING = 0.75
SPREAD = 0.75


def with_halo(block, sides, width):
    for axis, dim in sides:
        count = lax.axis_size(axis)
        forward = [(i, i + 1) for i in range(count - 1)]
        forward.append((count - 1, 0))
        backward = [(target, source) for source, target in forward]
        low = lax.ppermute(
            lax.slice_in_dim(block, block.shape[dim] - width, None, axis=dim), axis, forward
        )
        high = lax.ppermute(lax.slice_in_dim(block, 0, width, axis=dim), axis, backward)
        block = jnp.concatenate([low, block, high], axis=dim)
    return block


def silu_slope(values):
    sigmoid_part = jax.nn.sigmoid(values)
    return sigmoid_part * (1.0 + values * (1.0 - sigmoid_part))


def radial(source, target, factor, filters):
    square = jnp.zeros((source.shape[1], target.shape[1]), jnp.float32)
    for component in range(3):
        offset = source[component][:, None] - target[component][None, :]
        square = square + offset * offset
    distance = jnp.sqrt(square + 0.01)
    envelope = jnp.where(distance < CUTOFF, 0.5 * (jnp.cos(jnp.pi * distance / CUTOFF) + 1.0), 0.0)
    centers = jnp.arange(filters).astype(jnp.float32) * SPACING
    shifted = (distance[None] - centers[:, None, None]) / SPREAD
    return (jnp.exp(-shifted * shifted) * (envelope * factor)[None]).astype(jnp.bfloat16)


def body(
    atom_feat,
    atom_pos,
    atom_counts,
    atom_nbrs,
    probe_pos,
    probe_target,
    tile_blocks,
    atom_filter,
    probe_filter,
    mix_weight,
    readout,
):
    highest = lax.Precision.HIGHEST
    blocks_dev, channels, atom_width = atom_feat.shape
    tiles_dev, reads_tile = tile_blocks.shape
    probe_count = probe_pos.shape[2]
    filters = atom_filter.shape[1] // channels
    nbr_count = atom_nbrs.shape[1]
    tile_peers = lax.axis_size("tile")
    space_count = lax.axis_size("space")
    space_here = lax.axis_index("space")
    atom_mask = (jnp.arange(atom_width)[None, :] < atom_counts[:, None]).astype(jnp.float32)
    masked_feat = (atom_feat.astype(jnp.float32) * atom_mask[:, None, :]).astype(jnp.bfloat16)
    packed_rows = jnp.concatenate([masked_feat, atom_pos], axis=1)
    around_rows = with_halo(packed_rows, (("space", 0),), blocks_dev)
    side_index = (atom_nbrs // (tile_peers * blocks_dev) - space_here + 1) % space_count
    source_rows = side_index * blocks_dev + atom_nbrs % blocks_dev
    neighbour_rows = jnp.take(around_rows, source_rows.reshape(-1), axis=0).reshape(
        blocks_dev, nbr_count, channels + 3, atom_width
    )
    atom_scale = (nbr_count * atom_width) ** (-0.5)

    def atom_block(inputs):
        picked_rows, own_pos, own_feat, own_mask = inputs
        source_feat = picked_rows[:, :channels]
        source_where = picked_rows[:, channels:].astype(jnp.float32)
        target_where = own_pos.astype(jnp.float32)
        kernel_rows = jax.vmap(lambda source: radial(source, target_where, atom_scale, filters))(
            source_where
        )
        atom_sums = jnp.einsum(
            "kcj,krji->rci", source_feat, kernel_rows, preferred_element_type=jnp.float32
        )
        atom_sums = atom_sums.astype(jnp.bfloat16).reshape(filters * channels, atom_width)
        message = jnp.dot(atom_filter, atom_sums, preferred_element_type=jnp.float32)
        updated = (
            (own_feat.astype(jnp.float32) + jax.nn.silu(message)) * own_mask[None, :]
        ).astype(jnp.bfloat16)
        return (updated, atom_sums, message)

    updated, atom_sums, message = lax.map(
        atom_block, (neighbour_rows, atom_pos, atom_feat, atom_mask)
    )
    stored_rows = jnp.concatenate([updated, atom_pos], axis=1)
    flat_owner = (tile_blocks // blocks_dev % tile_peers).reshape(-1)
    flat_spot = (tile_blocks % blocks_dev).reshape(-1)
    request_cap = max(2, 2 * reads_tile * tiles_dev // tile_peers)
    matches = (flat_owner[:, None, None] == jnp.arange(tile_peers)[None, :, None]) & (
        flat_spot[:, None, None] == jnp.arange(blocks_dev)[None, None, :]
    )
    needed_rows = jnp.any(matches, axis=0).astype(jnp.int32)
    rank_rows = jnp.cumsum(needed_rows, axis=1) - needed_rows
    chosen_rows = (needed_rows[:, None, :] == 1) & (
        rank_rows[:, None, :] == jnp.arange(request_cap)[None, :, None]
    )
    request_ids = jnp.sum(
        chosen_rows.astype(jnp.int32) * jnp.arange(blocks_dev)[None, None, :], axis=2
    )
    asked_ids = lax.all_to_all(request_ids, "tile", split_axis=0, concat_axis=0, tiled=True)
    sent_rows = jnp.take(stored_rows, asked_ids, axis=0)
    replies, asked_ids = (
        lax.all_to_all(sent_rows, "tile", split_axis=0, concat_axis=0, tiled=True),
        asked_ids,
    )
    slot_index = flat_owner * request_cap + rank_rows[flat_owner, flat_spot]
    slot_total = tile_peers * request_cap
    fetched = jnp.take(replies.reshape(slot_total, channels + 3, atom_width), slot_index, axis=0)
    fetched = fetched.reshape(tiles_dev, reads_tile, channels + 3, atom_width)
    probe_scale = (reads_tile * atom_width) ** (-0.5)

    def probe_tile(tile_index):
        tile_fetch = fetched[tile_index]
        probe_where = probe_pos[tile_index]
        source_where = tile_fetch[:, channels:].astype(jnp.float32)
        kernels = jax.vmap(lambda source: radial(source, probe_where, probe_scale, filters))(
            source_where
        )
        summed = jnp.einsum(
            "kca,krap->rcp", tile_fetch[:, :channels], kernels, preferred_element_type=jnp.float32
        )
        summed = summed.astype(jnp.bfloat16).reshape(filters * channels, probe_count)
        hidden = jnp.dot(probe_filter, summed, preferred_element_type=jnp.float32)
        squashed = jax.nn.silu(hidden).astype(jnp.bfloat16)
        mixed_rows = jnp.dot(mix_weight, squashed, preferred_element_type=jnp.float32)
        outer_act = jax.nn.silu(mixed_rows)
        density = jnp.dot(readout, outer_act, precision=highest)
        misfit = (density - probe_target[tile_index]) / probe_count
        grad_readout = jnp.dot(outer_act, misfit, precision=highest)
        grad_mixed = (readout[:, None] * misfit[None, :] * silu_slope(mixed_rows)).astype(
            jnp.bfloat16
        )
        grad_mix = jnp.dot(grad_mixed, squashed.T, preferred_element_type=jnp.float32)
        grad_squashed = jnp.dot(mix_weight.T, grad_mixed, preferred_element_type=jnp.float32)
        grad_hidden = (grad_squashed * silu_slope(hidden)).astype(jnp.bfloat16)
        grad_probe = jnp.dot(grad_hidden, summed.T, preferred_element_type=jnp.float32)
        grad_summed = jnp.dot(probe_filter.T, grad_hidden, preferred_element_type=jnp.float32)
        grad_summed = grad_summed.astype(jnp.bfloat16).reshape(filters, channels, probe_count)
        grad_blocks = jnp.einsum(
            "rcp,krap->kca", grad_summed, kernels, preferred_element_type=jnp.float32
        )
        return (density, grad_probe, grad_mix, grad_readout, grad_blocks)

    density, grad_probe, grad_mix, grad_readout, grad_blocks = lax.map(
        probe_tile, jnp.arange(tiles_dev)
    )
    grad_flat = grad_blocks.reshape(tiles_dev * reads_tile, channels, atom_width)
    pick_rows = (slot_index[None, :] == jnp.arange(slot_total)[:, None]).astype(jnp.float32)
    slot_grad = jnp.einsum("gs,sca->gca", pick_rows, grad_flat, precision=highest).astype(
        jnp.bfloat16
    )
    returned = lax.all_to_all(
        slot_grad.reshape(tile_peers, request_cap, channels, atom_width),
        "tile",
        split_axis=0,
        concat_axis=0,
        tiled=True,
    )
    owner_pick = (asked_ids[:, :, None] == jnp.arange(blocks_dev)[None, None, :]).astype(
        jnp.float32
    )
    block_grad = jnp.einsum(
        "tkb,tkca->bca", owner_pick, returned.astype(jnp.float32), precision=highest
    )
    grad_message = (block_grad * atom_mask[:, None, :] * silu_slope(message)).astype(jnp.bfloat16)
    grad_atom = jnp.einsum(
        "bca,bda->cd", grad_message, atom_sums, preferred_element_type=jnp.float32
    )
    totals = lax.psum(
        (
            grad_atom,
            jnp.sum(grad_probe, axis=0),
            jnp.sum(grad_mix, axis=0),
            jnp.sum(grad_readout, axis=0),
        ),
        ("space", "tile"),
    )
    return (density, totals[0], totals[1], totals[2], totals[3])


def solution(mesh):
    return jax.shard_map(
        body,
        mesh=mesh,
        in_specs=(
            P(("space", "tile"), None, None),
            P(("space", "tile"), None, None),
            P(("space", "tile")),
            P(("space", "tile"), None),
            P(("space", "tile"), None, None),
            P(("space", "tile"), None),
            P(("space", "tile"), None),
            P(),
            P(),
            P(),
            P(),
        ),
        out_specs=(P(("space", "tile"), None), P(), P(), P(), P()),
        check_vma=False,
    )
```

profile of v0, /device:TPU:1, one launch (start us, length us, event | category | flops | bytes accessed | tf_op | source)
XLA Modules:
  0.0 433.1 jit_solution(2652389257295615800)
XLA Ops:
  14.2 5.6 %all-to-all-start = ((s32[8,1,4]{2,1,0:T(1,128)}), s32[8,1,4]{2,1,0:T(1,128)S(1)}, u32[]{:S(2)}, u32[]{:S(2)}) async-start(s32[8,1,4]{2,1,0:T(1,128)} %copy.115), calls=%async_computation | async-start | bytes 8192 | tf_op jit(solution)/shard_map/all_to_all | solution.py:111
  20.2 4.9 %all-to-all-done = s32[8,1,4]{2,1,0:T(1,128)S(1)} async-done(((s32[8,1,4]{2,1,0:T(1,128)}), s32[8,1,4]{2,1,0:T(1,128)S(1)}, u32[]{:S(2)}, u32[]{:S(2)}) %all-to-all-start) | async-done | bytes 160 | tf_op jit(solution)/shard_map/all_to_all | solution.py:111
  30.4 114.4 %while.36 = (s32[]{:T(128)}, bf16[16,128,128]{2,1,0:T(8,128)(2,1)S(1)}, bf16[16,1024,128]{2,1,0:T(8,128)(2,1)}, f32[16,128,128]{2,0,1:T(8,128)}, bf16[16,128,128...) while((s32[]{:T(128)}, ...), condition=%wide.region_4.5_spmd, body=%wide.region_3.4_spmd.sunk | while | flops 172165008 | bytes 3516337 | solution.py:93
  34.6 2.9 dynamic_update_slice.71
  41.8 2.9 dynamic_update_slice.71
  48.9 2.9 dynamic_update_slice.71
  56.1 2.9 dynamic_update_slice.71
  63.2 2.9 dynamic_update_slice.71
  70.4 2.9 dynamic_update_slice.71
  77.6 2.9 dynamic_update_slice.71
  84.7 2.9 dynamic_update_slice.71
  91.9 2.9 dynamic_update_slice.71
  99.1 2.9 dynamic_update_slice.71
  106.2 2.9 dynamic_update_slice.71
  113.4 2.9 dynamic_update_slice.71
  120.5 2.9 dynamic_update_slice.71
  127.6 2.9 dynamic_update_slice.71
  134.8 2.9 dynamic_update_slice.71
  141.9 2.9 dynamic_update_slice.71
  147.8 5.0 %all-to-all-start.1 = ((bf16[8,4,131,128]{3,1,2,0:T(4,128)(2,1)}), bf16[8,4,131,128]{3,1,2,0:T(4,128)(2,1)S(1)}, u32[]{:S(2)}, u32[]{:S(2)}) async-start(bf16[8,4,131,128]{3,1,2,0:T(4,128)(2,1)} %copy.129), calls=%async_computation.1 | async-start | bytes 2146304 | tf_op jit(solution)/shard_map/all_to_all | solution.py:114
  154.3 23.5 %all-to-all-done.1 = bf16[8,4,131,128]{3,1,2,0:T(4,128)(2,1)S(1)} async-done(((bf16[8,4,131,128]{3,1,2,0:T(4,128)(2,1)}), bf16[8,4,131,128]{3,1,2,0:T(4,128)(2,1)S(1)}, u32[]{:S(2)}, u32[]{:S(2)}) %all-to-all-start.1) | async-done | bytes 1073184 | tf_op jit(solution)/shard_map/all_to_all | solution.py:114
  179.6 70.1 %while.37 = (s32[]{:T(128)}, f32[2,512]{1,0:T(2,128)S(1)}, f32[2,128,1024]{2,1,0:T(8,128)}, f32[2,128,128]{2,1,0:T(8,128)}, f32[2,128]{1,0:T(2,128)}, /*index=5*...) while((s32[]{:T(128)}, f32[2,512]{1,0:T(2,128)S(1)}, ...), condition=%wide.region_6.7_spmd, body=%wide.region_5.6_spmd.sunk | while | flops 2663714816 | bytes 38164880 | solution.py:155
  183.3 8.5 %add_sqrt_fusion.5 = (f32[8,128,512]{2,1,0:T(8,128)S(1)}, f32[8,128,512]{2,1,0:T(8,128)S(1)}) fusion(f32[512]{0:T(512)S(1)} %bitcast.288, f32[8,128]{1,0:T(8,128)S(1)} %bitcast.284, f32[512]{0:T(512)S(1)} %bitcast.287, f32[8,128]{1,0:T(8,128)S(1)} %bitcast.285, f32[512]{0:T(512)S(1)} %bitcast.286, f32[8,128]{1,0:T(8,128)S(1)} %bitcast.283), kind=kLoop, calls=%fused_computation.47.clone.2 | loop fusion | flops 7864320 | bytes 4212736 | tf_op jit(solution)/shard_map/while/body/eval_jaxpr/vmap()/sqrt | solution.py:35
  191.9 5.1 %bitcast_convert_fusion.2 = bf16[8,512,128]{1,2,0:T(8,128)(2,1)S(1)} fusion(f32[8,128,512]{2,1,0:T(8,128)S(1)} %get-tuple-element.580, f32[8]{0:T(128)S(1)} %convert_multiply_fusion.5, f32[8,128,512]{2,1,0:T(8,128)S(1)} %get-tuple-element.581, bf16[8,131,128]{2,1,0:T(8,128)(2,1)S(1)} %dynamic-slice_bitcast_fusion.5), kind=kOutput, calls=%fused_computation.45.clone.1 | convolution fusion | flops 1099431936 | bytes 5505536 | tf_op jit(solution)/shard_map/while/body/eval_jaxpr/kca,krap->rcp/dot_general | solution.py:130
  207.6 7.0 %fusion.163 = f32[2,8,128,128]{2,3,1,0:T(8,128)} fusion(f32[2,8,128,128]{2,3,1,0:T(8,128)} %get-tuple-element.638, s32[]{:T(128)S(6)} %copy.188, bf16[8,128,512,1]{2,1,0,3:T(8,128)(2,1)} %bitcast.273, f32[8,128,512]{2,1,0:T(8,128)} %copy-done, f32[8]{0:T(128)} %copy-done.31, f32[8,128,512]{2,1,0:T(8,128)S(1)} %get-tuple-element.581), kind=kOutput, calls=%fused_computation.51.clone.1 | convolution fusion | flops 1098907648 | bytes 5767684 | tf_op jit(solution)/shard_map/while/body/eval_jaxpr/rcp,krap->kca/dot_general | solution.py:150
  218.2 8.5 %add_sqrt_fusion.5 = (f32[8,128,512]{2,1,0:T(8,128)S(1)}, f32[8,128,512]{2,1,0:T(8,128)S(1)}) fusion(f32[512]{0:T(512)S(1)} %bitcast.288, f32[8,128]{1,0:T(8,128)S(1)} %bitcast.284, f32[512]{0:T(512)S(1)} %bitcast.287, f32[8,128]{1,0:T(8,128)S(1)} %bitcast.285, f32[512]{0:T(512)S(1)} %bitcast.286, f32[8,128]{1,0:T(8,128)S(1)} %bitcast.283), kind=kLoop, calls=%fused_computation.47.clone.2 | loop fusion | flops 7864320 | bytes 4212736 | tf_op jit(solution)/shard_map/while/body/eval_jaxpr/vmap()/sqrt | solution.py:35
  226.7 5.1 %bitcast_convert_fusion.2 = bf16[8,512,128]{1,2,0:T(8,128)(2,1)S(1)} fusion(f32[8,128,512]{2,1,0:T(8,128)S(1)} %get-tuple-element.580, f32[8]{0:T(128)S(1)} %convert_multiply_fusion.5, f32[8,128,512]{2,1,0:T(8,128)S(1)} %get-tuple-element.581, bf16[8,131,128]{2,1,0:T(8,128)(2,1)S(1)} %dynamic-slice_bitcast_fusion.5), kind=kOutput, calls=%fused_computation.45.clone.1 | convolution fusion | flops 1099431936 | bytes 5505536 | tf_op jit(solution)/shard_map/while/body/eval_jaxpr/kca,krap->rcp/dot_general | solution.py:130
  242.4 7.0 %fusion.163 = f32[2,8,128,128]{2,3,1,0:T(8,128)} fusion(f32[2,8,128,128]{2,3,1,0:T(8,128)} %get-tuple-element.638, s32[]{:T(128)S(6)} %copy.188, bf16[8,128,512,1]{2,1,0,3:T(8,128)(2,1)} %bitcast.273, f32[8,128,512]{2,1,0:T(8,128)} %copy-done, f32[8]{0:T(128)} %copy-done.31, f32[8,128,512]{2,1,0:T(8,128)S(1)} %get-tuple-element.581), kind=kOutput, calls=%fused_computation.51.clone.1 | convolution fusion | flops 1098907648 | bytes 5767684 | tf_op jit(solution)/shard_map/while/body/eval_jaxpr/rcp,krap->kca/dot_general | solution.py:150
  254.0 5.2 %all-to-all-start.2 = ((bf16[8,4,128,128]{3,1,2,0:T(4,128)(2,1)}), bf16[8,4,128,128]{3,1,2,0:T(4,128)(2,1)S(1)}, u32[]{:S(2)}, u32[]{:S(2)}) async-start(bf16[8,4,128,128]{3,1,2,0:T(4,128)(2,1)} %copy.133), calls=%async_computation.2 | async-start | bytes 2097152 | tf_op jit(solution)/shard_map/all_to_all | solution.py:163
  260.9 23.4 %all-to-all-done.2 = bf16[8,4,128,128]{3,1,2,0:T(4,128)(2,1)S(1)} async-done(((bf16[8,4,128,128]{3,1,2,0:T(4,128)(2,1)}), bf16[8,4,128,128]{3,1,2,0:T(4,128)(2,1)S(1)}, u32[]{:S(2)}, u32[]{:S(2)}) %all-to-all-start.2) | async-done | bytes 1048608 | tf_op jit(solution)/shard_map/all_to_all | solution.py:163
  288.7 39.6 %psum.31 = f32[128]{0:T(128)} all-reduce(f32[128]{0:T(128)S(1)} %reduce_sum.39), channel_id=1, replica_groups=mesh['space'=4,'tile'=8] {'space','tile'}, use_global_device_ids=true, to_apply=%region_13.14 | all-reduce | flops 128 | bytes 1024 | tf_op jit(solution)/shard_map/psum | solution.py:180
  328.3 93.5 %all-reduce.3.cloned.1.call-done = (f32[128,1024]{1,0:T(8,128)}, f32[128,1024]{1,0:T(8,128)}, f32[128,128]{1,0:T(8,128)}) async-done(((f32[128,1024]{1,0:T(8,128)}, f32[128,1024]{1,0:T(8,128)}, f32[128,128]{1,0:T(8,128)}), (f32[128,1024]{1,0:T(8,128)}, f32[128,1024]{1,0:T(8,128)}, f32[128,128]{1,0:T(8,128)})) %all-reduce.3.cloned.1.call-update) | async-done | bytes 1114128 | tf_op jit(solution)/shard_map/psum | solution.py:180
  (480 shorter events, 123.7 us)
Async XLA Ops:
  7.2 12.6 %copy-start.10 = (bf16[16,3,128]{2,0,1:T(8,128)(2,1)S(1)}, bf16[16,3,128]{2,0,1:T(8,128)(2,1)}, u32[]{:S(2)}) copy-start(bf16[16,3,128]{2,0,1:T(8,128)(2,1)} %param.16) | copy-start | bytes 36868
  7.2 5.6 %copy-start.18 = (s32[2,8]{1,0:T(2,128)S(1)}, s32[2,8]{1,0:T(2,128)}, u32[]{:S(2)}) copy-start(s32[2,8]{1,0:T(2,128)} %param.21) | copy-start | bytes 196
  7.2 12.6 %copy-start.17 = (s32[16,4]{0,1:T(4,128)S(1)}, s32[16,4]{0,1:T(4,128)}, u32[]{:S(2)}) copy-start(s32[16,4]{0,1:T(4,128)} %param.18) | copy-start | bytes 772
  10.1 15.4 %collective-permute-start.1 = (bf16[16,131,128]{2,0,1:T(8,128)(2,1)S(1)}, bf16[16,131,128]{2,0,1:T(8,128)(2,1)S(1)}, u32[]{:S(2)}, u32[]{:S(2)}) collective-permute-start(bf16[16,131,128]{2,0,1:T(8,128)(2,1)S(1)} %pad_maximum_fusion.2), channel_id=1, source_target_pairs={{8,0},{16,8},{24,16},{0,24},{9,1},{17,9},{25,17},{1,25},{10,2},{18... | collective-permute-start | bytes 1609736 | tf_op jit(solution)/shard_map/ppermute | solution.py:20
  10.1 15.3 %collective-permute-start = (bf16[16,131,128]{2,0,1:T(8,128)(2,1)S(1)}, bf16[16,131,128]{2,0,1:T(8,128)(2,1)S(1)}, u32[]{:S(2)}, u32[]{:S(2)}) collective-permute-start(bf16[16,131,128]{2,0,1:T(8,128)(2,1)S(1)} %pad_maximum_fusion.2), channel_id=1, source_target_pairs={{0,8},{8,16},{16,24},{24,0},{1,9},{9,17},{17,25},{25,1},{2,10},{10... | collective-permute-start | bytes 1609736 | tf_op jit(solution)/shard_map/ppermute | solution.py:17
  14.2 10.8 %all-to-all-start = ((s32[8,1,4]{2,1,0:T(1,128)}), s32[8,1,4]{2,1,0:T(1,128)S(1)}, u32[]{:S(2)}, u32[]{:S(2)}) async-start(s32[8,1,4]{2,1,0:T(1,128)} %copy.115), calls=%async_computation | async-start | bytes 8192 | tf_op jit(solution)/shard_map/all_to_all | solution.py:111
  147.8 30.0 %all-to-all-start.1 = ((bf16[8,4,131,128]{3,1,2,0:T(4,128)(2,1)}), bf16[8,4,131,128]{3,1,2,0:T(4,128)(2,1)S(1)}, u32[]{:S(2)}, u32[]{:S(2)}) async-start(bf16[8,4,131,128]{3,1,2,0:T(4,128)(2,1)} %copy.129), calls=%async_computation.1 | async-start | bytes 2146304 | tf_op jit(solution)/shard_map/all_to_all | solution.py:114
  154.2 25.3 %copy-start.1 = (bf16[128,1024]{1,0:T(8,128)(2,1)S(1)}, bf16[128,1024]{1,0:T(8,128)(2,1)}, u32[]{:S(2)}) copy-start(bf16[128,1024]{1,0:T(8,128)(2,1)} %param.23) | copy-start | bytes 786436
  154.2 25.3 %copy-start.11 = (f32[2,3,512]{2,0,1:T(2,128)S(1)}, f32[2,3,512]{2,0,1:T(2,128)}, u32[]{:S(2)}) copy-start(f32[2,3,512]{2,0,1:T(2,128)} %param.19) | copy-start | bytes 36868
  154.2 25.3 %copy-start.15 = (f32[128]{0:T(128)S(1)}, f32[128]{0:T(128)}, u32[]{:S(2)}) copy-start(f32[128]{0:T(128)} %param.25) | copy-start | bytes 1540
  154.3 25.3 %copy-start.24 = (bf16[128,128]{1,0:T(8,128)(2,1)S(1)}, bf16[128,128]{1,0:T(8,128)(2,1)}, u32[]{:S(2)}) copy-start(bf16[128,128]{1,0:T(8,128)(2,1)} %param.24) | copy-start | bytes 98308
  179.7 12.1 %copy-start.29 = (s32[2]{0:T(128)}, s32[2]{0:T(128)S(1)}, u32[]{:S(2)}) copy-start(s32[2]{0:T(128)S(1)} %get-tuple-element.657) | copy-start | bytes 28 | tf_op jit(solution)/shard_map/while
  191.8 5.2 %copy-start = (f32[8,128,512]{2,1,0:T(8,128)}, f32[8,128,512]{2,1,0:T(8,128)S(1)}, u32[]{:S(2)}) copy-start(f32[8,128,512]{2,1,0:T(8,128)S(1)} %get-tuple-element.580) | copy-start | bytes 6291460 | tf_op jit(solution)/shard_map/while
  191.9 5.2 %copy-start.31 = (f32[8]{0:T(128)}, f32[8]{0:T(128)S(1)}, u32[]{:S(2)}) copy-start(f32[8]{0:T(128)S(1)} %convert_multiply_fusion.5) | copy-start | bytes 100 | tf_op jit(solution)/shard_map/while
  199.6 4.4 %copy-start.6 = (f32[128,512]{0,1:T(8,128)S(1)}, f32[128,512]{0,1:T(8,128)}, u32[]{:S(2)}) copy-start(f32[128,512]{0,1:T(8,128)} %copy-done.5) | copy-start | bytes 786436 | tf_op jit(solution)/shard_map/while
  207.6 7.0 %copy-start.16 = (f32[128]{0:T(128)S(1)}, f32[128]{0:T(128)}, u32[]{:S(2)}) copy-start(f32[128]{0:T(128)} %get-tuple-element.715) | copy-start | bytes 1540 | tf_op jit(solution)/shard_map/while
  207.6 7.0 %copy-start.25 = (bf16[128,128]{1,0:T(8,128)(2,1)S(1)}, bf16[128,128]{1,0:T(8,128)(2,1)}, u32[]{:S(2)}) copy-start(bf16[128,128]{1,0:T(8,128)(2,1)} %get-tuple-element.735) | copy-start | bytes 98308 | tf_op jit(solution)/shard_map/while
  207.6 7.0 %copy-start.27 = (f32[2,512]{1,0:T(2,128)S(1)}, f32[2,512]{1,0:T(2,128)}, u32[]{:S(2)}) copy-start(f32[2,512]{1,0:T(2,128)} %copy-done.26) | copy-start | bytes 12292 | tf_op jit(solution)/shard_map/while
  207.6 7.0 %copy-start.30 = (s32[2]{0:T(128)S(1)}, s32[2]{0:T(128)}, u32[]{:S(2)}) copy-start(s32[2]{0:T(128)} %copy-done.29) | copy-start | bytes 28 | tf_op jit(solution)/shard_map/while
  214.6 12.1 %copy-start.29 = (s32[2]{0:T(128)}, s32[2]{0:T(128)S(1)}, u32[]{:S(2)}) copy-start(s32[2]{0:T(128)S(1)} %get-tuple-element.657) | copy-start | bytes 28 | tf_op jit(solution)/shard_map/while
  226.7 5.2 %copy-start = (f32[8,128,512]{2,1,0:T(8,128)}, f32[8,128,512]{2,1,0:T(8,128)S(1)}, u32[]{:S(2)}) copy-start(f32[8,128,512]{2,1,0:T(8,128)S(1)} %get-tuple-element.580) | copy-start | bytes 6291460 | tf_op jit(solution)/shard_map/while
  226.7 5.2 %copy-start.31 = (f32[8]{0:T(128)}, f32[8]{0:T(128)S(1)}, u32[]{:S(2)}) copy-start(f32[8]{0:T(128)S(1)} %convert_multiply_fusion.5) | copy-start | bytes 100 | tf_op jit(solution)/shard_map/while
  242.4 7.0 %copy-start.16 = (f32[128]{0:T(128)S(1)}, f32[128]{0:T(128)}, u32[]{:S(2)}) copy-start(f32[128]{0:T(128)} %get-tuple-element.715) | copy-start | bytes 1540 | tf_op jit(solution)/shard_map/while
  242.4 7.0 %copy-start.25 = (bf16[128,128]{1,0:T(8,128)(2,1)S(1)}, bf16[128,128]{1,0:T(8,128)(2,1)}, u32[]{:S(2)}) copy-start(bf16[128,128]{1,0:T(8,128)(2,1)} %get-tuple-element.735) | copy-start | bytes 98308 | tf_op jit(solution)/shard_map/while
  242.4 7.0 %copy-start.27 = (f32[2,512]{1,0:T(2,128)S(1)}, f32[2,512]{1,0:T(2,128)}, u32[]{:S(2)}) copy-start(f32[2,512]{1,0:T(2,128)} %copy-done.26) | copy-start | bytes 12292 | tf_op jit(solution)/shard_map/while
  242.4 7.0 %copy-start.30 = (s32[2]{0:T(128)S(1)}, s32[2]{0:T(128)}, u32[]{:S(2)}) copy-start(s32[2]{0:T(128)} %copy-done.29) | copy-start | bytes 28 | tf_op jit(solution)/shard_map/while
  252.5 6.8 %copy-start.8 = (f32[2,128,1024]{2,1,0:T(8,128)S(1)}, f32[2,128,1024]{2,1,0:T(8,128)}, u32[]{:S(2)}) copy-start(f32[2,128,1024]{2,1,0:T(8,128)} %get-tuple-element.718) | copy-start | bytes 3145732
  254.0 6.2 %copy-start.9 = (f32[2,128,128]{2,1,0:T(8,128)S(1)}, f32[2,128,128]{2,1,0:T(8,128)}, u32[]{:S(2)}) copy-start(f32[2,128,128]{2,1,0:T(8,128)} %get-tuple-element.719) | copy-start | bytes 393220
  254.0 30.2 %copy-start.14 = (f32[16,128]{1,0:T(8,128)S(1)}, f32[16,128]{1,0:T(8,128)}, u32[]{:S(2)}) copy-start(f32[16,128]{1,0:T(8,128)} %copy-done.13) | copy-start | bytes 24580
  254.0 30.2 %copy-start.23 = (f32[16,128,128]{2,0,1:T(8,128)S(1)}, f32[16,128,128]{2,0,1:T(8,128)}, u32[]{:S(2)}) copy-start(f32[16,128,128]{2,0,1:T(8,128)} %get-tuple-element.288) | copy-start | bytes 3145732
  254.0 30.2 %all-to-all-start.2 = ((bf16[8,4,128,128]{3,1,2,0:T(4,128)(2,1)}), bf16[8,4,128,128]{3,1,2,0:T(4,128)(2,1)S(1)}, u32[]{:S(2)}, u32[]{:S(2)}) async-start(bf16[8,4,128,128]{3,1,2,0:T(4,128)(2,1)} %copy.133), calls=%async_computation.2 | async-start | bytes 2097152 | tf_op jit(solution)/shard_map/all_to_all | solution.py:163
  259.2 162.7 %all-reduce.3.cloned.1.call-start = ((), (), s32[]{:S(2)}) async-start(), calls=%async_computation.3 | async-start | bytes 2228224 | tf_op jit(solution)/shard_map/psum | solution.py:180
  (20 other events, 34.9 us)
Sparse Core Ops, SparseCore 0:
  288.8 132.9 all-reduce.2
where the time goes:
time: 436 us; the launch traced here: 433 us
  waiting for transfers between devices  145 us (33%)
  local copies, waits for them, and re-layouts  105 us (24%)
  matrix products  55.9 us (13%)
  other arithmetic  47.9 us (11%)
  blocking collectives  39.6 us (9%)
  starting transfers between devices  18.4 us (4%)
  between operations  14.4 us (3%)
  loops' own time  6.15 us (1%)
    psum x1, waiting for transfers between devices, body(): lax.psum((grad_atom, jnp.sum(grad_probe, axis=0), jnp.sum(grad_mix, axis=...  93.5 us
    dynamic_update_slice x80, local copies, waits for them, and re-layouts, body(): lax.map(atom_block, (neighbour_rows, atom_pos, atom_feat, atom_mask))  62.2 us
    psum x1, blocking collectives, body(): lax.psum((grad_atom, jnp.sum(grad_probe, axis=0), jnp.sum(grad_mix, axis=...  39.6 us
    sqrt x18, other arithmetic, radial(): distance = jnp.sqrt(square + 0.01)  34.7 us
    all_to_all x1, waiting for transfers between devices, body(): lax.all_to_all(sent_rows, 'tile', split_axis=0, concat_axis=0, tiled=True)  23.5 us
    all_to_all x1, waiting for transfers between devices, body(): lax.all_to_all(slot_grad.reshape(tile_peers, request_cap, channels, atom_...  23.4 us
    dynamic_slice x32, local copies, waits for them, and re-layouts, body(): lax.map(atom_block, (neighbour_rows, atom_pos, atom_feat, atom_mask))  14 us
    dot_general x2, matrix products, probe_tile(): jnp.einsum('rcp,krap->kca', grad_summed, kernels, preferred_element_type=...  14 us
  transfers between devices with their start and end apart: 6, of which 4 were waited for; matrix products, arithmetic and copies ran while one was open for 1% of the time, Pallas kernels for 0%

commit v1 on v0

v1 whole, which is shorter than its diff:
```python
import functools
import math

import jax
import jax.numpy as jnp
from jax import lax
from jax.experimental import pallas as pl
from jax.experimental.pallas import tpu as pltpu
from jax.sharding import PartitionSpec as P

CUTOFF = 6.0
SPACING = 0.75
SPREAD = 0.75
LOG2E = 1.4426950408889634
MESH = pl.DeviceIdType.MESH
VMEM_LIMIT = 56 * 1024 * 1024
F32 = jnp.float32
BF16 = jnp.bfloat16


def silu_slope(values):
    s = jax.nn.sigmoid(values)
    return s * (1.0 + values * (1.0 - s))


def radial(source_cols, target_rows, factor, filters):
    square = None
    for source, target in zip(source_cols, target_rows):
        offset = source - target
        square = offset * offset if square is None else square + offset * offset
    square = square + 0.01
    distance = square * lax.rsqrt(square)
    half = (math.pi / (2.0 * CUTOFF)) ** 2
    terms = [math.sqrt(factor) * (-half) ** k / math.factorial(2 * k) for k in range(7)]
    wave = terms[6] * square + terms[5]
    for term in terms[4::-1]:
        wave = wave * square + term
    envelope = jnp.where(square < CUTOFF * CUTOFF, wave * wave, 0.0)
    middle = filters // 2
    shifted = distance * (1.0 / SPREAD) - middle * (SPACING / SPREAD)
    step = SPACING / SPREAD
    centre = envelope * jnp.exp2(shifted * shifted * (-LOG2E))
    ratio = 2.0 * step * LOG2E
    up = jnp.exp2(shifted * ratio - step * step * LOG2E)
    down = jnp.exp2(shifted * (-ratio) - step * step * LOG2E)
    values = [None] * filters
    values[middle] = centre
    now = centre
    for k in range(filters - 1 - middle):
        now = now * (up if k == 0 else up * math.exp(-2.0 * k * step * step))
        values[middle + k + 1] = now
    now = centre
    for k in range(middle):
        now = now * (down if k == 0 else down * math.exp(-2.0 * k * step * step))
        values[middle - k - 1] = now
    return values


def dot(a, b):
    return jnp.dot(a, b, preferred_element_type=F32)


def dot_nt(a, b):
    return lax.dot_general(a, b, (((1,), (1,)), ((), ())), preferred_element_type=F32)


def atom_kernel(
    rows_ref, around_ref, where_ref, own_feat_ref, own_where_ref, filter_ref,
    stored_ref, sums_ref, message_ref, columns, radial_rows, feats,
):
    block = pl.program_id(0)
    channels, width = own_feat_ref.shape[1:]
    filters = filter_ref.shape[1] // channels
    nbrs = feats.shape[1] // width
    factor = (nbrs * width) ** (-0.5)
    own = own_where_ref[0].astype(F32)
    target = [own[c : c + 1, :] for c in range(3)]
    for k in range(nbrs):
        row = rows_ref[block * nbrs + k]
        where = where_ref[row].astype(F32)
        columns[k * width : (k + 1) * width, :] = where[:8].T
        keep = jnp.broadcast_to(where[3:4, :], (channels, width)) > 0.5
        feats[:, k * width : (k + 1) * width] = jnp.where(
            keep, around_ref[row].astype(F32), 0.0
        ).astype(BF16)
    chunk = 32

    def fill(step, carry):
        start = pl.multiple_of(step * chunk, chunk)
        source = [columns[pl.ds(start, chunk), c : c + 1] for c in range(3)]
        for r, value in enumerate(radial(source, target, factor, filters)):
            radial_rows[pl.ds(start, chunk), r * width : (r + 1) * width] = value.astype(BF16)
        return carry

    lax.fori_loop(0, nbrs * width // chunk, fill, 0, unroll=2)
    total = dot(feats[...], radial_rows[...]).astype(BF16)
    for r in range(filters):
        sums_ref[0, r * channels : (r + 1) * channels, :] = total[:, r * width : (r + 1) * width]
    message = dot(filter_ref[...], sums_ref[0])
    message_ref[0] = message
    updated = (own_feat_ref[0].astype(F32) + message * jax.nn.sigmoid(message)) * own[3:4, :]
    stored_ref[0, :channels, :] = updated.astype(BF16)
    stored_ref[0, channels:, :] = own_where_ref[0]


def probe_kernel(
    slots_ref, replies_ref, where_ref, target_ref, filter_ref, mix_ref, readout_ref,
    density_ref, grad_filter_ref, grad_mix_ref, grad_readout_ref, slot_grad_ref,
    columns, radial_rows, feats, summed, turned, slot_total,
):
    tile = pl.program_id(0)
    tiles = pl.num_programs(0)
    channels = mix_ref.shape[0]
    filters = filter_ref.shape[1] // channels
    width = replies_ref.shape[2]
    reads = feats.shape[1] // width
    probes = where_ref.shape[2]
    factor = (reads * width) ** (-0.5)

    @pl.when(tile == 0)
    def _():
        slot_total[...] = jnp.zeros_like(slot_total)
        grad_filter_ref[...] = jnp.zeros_like(grad_filter_ref)
        grad_mix_ref[...] = jnp.zeros_like(grad_mix_ref)
        grad_readout_ref[...] = jnp.zeros_like(grad_readout_ref)

    for k in range(reads):
        slot = slots_ref[tile * reads + k]
        row = replies_ref[slot]
        columns[k * width : (k + 1) * width, :] = row[channels:].astype(F32)[:8].T
        feats[:, k * width : (k + 1) * width] = row[:channels]
    chunk, span = 16, 256
    lanes = []
    for p in range(0, probes, span):
        lanes.append([where_ref[0, c : c + 1, p : p + span] for c in range(3)])

    def fill(step, carry):
        start = pl.multiple_of(step * chunk, chunk)
        source = [columns[pl.ds(start, chunk), c : c + 1] for c in range(3)]
        for n, target in enumerate(lanes):
            for r, value in enumerate(radial(source, target, factor, filters)):
                low = r * probes + n * span
                radial_rows[pl.ds(start, chunk), low : low + span] = value.astype(BF16)
        return carry

    lax.fori_loop(0, reads * width // chunk, fill, 0)
    for r in range(filters):
        summed[r * channels : (r + 1) * channels, :] = dot(
            feats[...], radial_rows[:, r * probes : (r + 1) * probes]
        ).astype(BF16)
    hidden = dot(filter_ref[...], summed[...])
    gate = jax.nn.sigmoid(hidden)
    squashed = (hidden * gate).astype(BF16)
    mixed = dot(mix_ref[...], squashed)
    mixed_gate = jax.nn.sigmoid(mixed)
    outer = mixed * mixed_gate
    readout = jnp.broadcast_to(readout_ref[...], (8, channels)).T[:, :1]
    density = jnp.sum(readout * outer, axis=0, keepdims=True)
    density_ref[0] = density
    misfit = (density - target_ref[0]) / probes
    part = jnp.sum(outer * misfit, axis=1, keepdims=True)
    grad_readout_ref[...] += jnp.broadcast_to(part, (channels, channels)).T[:8, :]
    grad_mixed = (
        readout * misfit * (mixed_gate * (1.0 + mixed * (1.0 - mixed_gate)))
    ).astype(BF16)
    grad_mix_ref[...] += dot_nt(grad_mixed, squashed)
    grad_squashed = dot(mix_ref[...].T, grad_mixed)
    grad_hidden = (grad_squashed * (gate * (1.0 + hidden * (1.0 - gate)))).astype(BF16)
    grad_filter_ref[...] += dot_nt(grad_hidden, summed[...])
    grad_sums = dot(grad_hidden.T, filter_ref[...]).astype(BF16)
    for r in range(filters):
        turned[r * probes : (r + 1) * probes, :] = grad_sums[:, r * channels : (r + 1) * channels]
    for k in range(reads):
        slot = slots_ref[tile * reads + k]
        back = dot(radial_rows[k * width : (k + 1) * width, :], turned[...])
        slot_total[slot] += back.T

    @pl.when(tile == tiles - 1)
    def _():
        slot_grad_ref[...] = slot_total[...].astype(BF16)


def final_kernel(ids_ref, returned_ref, where_ref, message_ref, sums_ref, grad_ref, totals):
    block = pl.program_id(0)

    @pl.when(block == 0)
    def _():
        totals[...] = jnp.zeros_like(totals)
        grad_ref[...] = jnp.zeros_like(grad_ref)

        def add(slot, carry):
            totals[ids_ref[slot]] += returned_ref[slot].astype(F32)
            return carry

        lax.fori_loop(0, returned_ref.shape[0], add, 0)

    keep = where_ref[0].astype(F32)[3:4, :]
    grad_message = (totals[block] * keep * silu_slope(message_ref[0])).astype(BF16)
    grad_ref[...] += dot_nt(grad_message, sums_ref[0])


def reduce_kernel(
    axes, atom_ref, filter_ref, mix_ref, readout_ref,
    atom_out, filter_out, mix_out, readout_out,
    total, sending, landing, gathered, send_sems, recv_sems,
):
    channels = atom_ref.shape[0]
    filters = atom_ref.shape[1] // channels
    rows = total.shape[0]
    partners = []
    for axis, size in axes:
        here = lax.axis_index(axis)
        bit = 1
        while bit < size:
            side = (here // bit) % 2
            partners.append((axis, here + bit * (1 - 2 * side), side))
            bit *= 2
    barrier = pltpu.get_barrier_semaphore()
    for axis, other, _ in partners:
        pl.semaphore_signal(barrier, inc=1, device_id={axis: other}, device_id_type=MESH)
    for r in range(filters):
        total[r * channels : (r + 1) * channels, :] = atom_ref[:, r * channels : (r + 1) * channels]
        low = (filters + r) * channels
        total[low : low + channels, :] = filter_ref[:, r * channels : (r + 1) * channels]
    low = 2 * filters * channels
    total[low : low + channels, :] = mix_ref[...]
    total[low + channels : low + channels + 8, :] = readout_ref[...]
    total[low + channels + 8 :, :] = jnp.zeros((rows - low - channels - 8, channels), F32)
    pl.semaphore_wait(barrier, len(partners))
    start = 0
    size = rows
    place = 0
    copies = []
    ranges = []
    for n, (axis, other, side) in enumerate(partners):
        size //= 2
        keep = pl.multiple_of(start + side * size, 16)
        give = pl.multiple_of(start + (1 - side) * size, 16)
        sending[place : place + size, :] = total[pl.ds(give, size), :].astype(BF16)
        copy = pltpu.make_async_remote_copy(
            src_ref=sending.at[pl.ds(place, size)],
            dst_ref=landing.at[pl.ds(place, size)],
            send_sem=send_sems.at[n],
            recv_sem=recv_sems.at[n],
            device_id={axis: other},
            device_id_type=MESH,
        )
        copy.start()
        copy.wait_recv()
        total[pl.ds(keep, size), :] += landing[place : place + size, :].astype(F32)
        copies.append(copy)
        ranges.append((keep, size))
        place += size
        start = keep
    keep, size = ranges[-1]
    gathered[pl.ds(keep, size), :] = total[pl.ds(keep, size), :].astype(BF16)
    for n in range(len(partners) - 1, -1, -1):
        axis, other, _ = partners[n]
        keep, size = ranges[n]
        copy = pltpu.make_async_remote_copy(
            src_ref=gathered.at[pl.ds(keep, size)],
            dst_ref=gathered.at[pl.ds(keep, size)],
            send_sem=send_sems.at[len(partners) + n],
            recv_sem=recv_sems.at[len(partners) + n],
            device_id={axis: other},
            device_id_type=MESH,
        )
        copy.start()
        copy.wait_recv()
        copies.append(copy)
    for r in range(filters):
        atom_out[:, r * channels : (r + 1) * channels] = gathered[
            r * channels : (r + 1) * channels, :
        ].astype(F32)
        low = (filters + r) * channels
        filter_out[:, r * channels : (r + 1) * channels] = gathered[low : low + channels, :].astype(F32)
    low = 2 * filters * channels
    mix_out[...] = gathered[low : low + channels, :].astype(F32)
    readout_out[...] = gathered[low + channels : low + channels + 16, :].astype(F32)[:8, :]
    for copy in copies:
        copy.wait_send()


def whole(array):
    return pl.BlockSpec(array.shape, lambda *_: (0,) * array.ndim)


def body(
    atom_feat, atom_pos, atom_counts, atom_nbrs, probe_pos, probe_target, tile_blocks,
    atom_filter, probe_filter, mix_weight, readout,
):
    blocks, channels, width = atom_feat.shape
    tiles, reads = tile_blocks.shape
    probes = probe_pos.shape[2]
    filters = atom_filter.shape[1] // channels
    nbrs = atom_nbrs.shape[1]
    peers = lax.axis_size("tile")
    space_count = lax.axis_size("space")
    here = lax.axis_index("space")
    params = pltpu.CompilerParams(vmem_limit_bytes=VMEM_LIMIT)
    mask = (jnp.arange(width)[None, :] < atom_counts[:, None]).astype(BF16)
    where = jnp.concatenate(
        [atom_pos, mask[:, None, :], jnp.zeros((blocks, 12, width), BF16)], axis=1
    )
    forward = [(i, (i + 1) % space_count) for i in range(space_count)]
    backward = [(b, a) for a, b in forward]
    around_feat = jnp.concatenate(
        [
            lax.ppermute(atom_feat, "space", forward),
            atom_feat,
            lax.ppermute(atom_feat, "space", backward),
        ],
        axis=0,
    )
    around_where = jnp.concatenate(
        [
            lax.ppermute(where, "space", forward),
            where,
            lax.ppermute(where, "space", backward),
        ],
        axis=0,
    )
    side = (atom_nbrs // (peers * blocks) - here + 1) % space_count
    source_rows = (side * blocks + atom_nbrs % blocks).reshape(-1)

    flat_owner = (tile_blocks // blocks % peers).reshape(-1)
    flat_spot = (tile_blocks % blocks).reshape(-1)
    cap = max(2, 2 * reads * tiles // peers)
    matches = (flat_owner[:, None, None] == jnp.arange(peers)[None, :, None]) & (
        flat_spot[:, None, None] == jnp.arange(blocks)[None, None, :]
    )
    needed = jnp.any(matches, axis=0).astype(jnp.int32)
    rank = jnp.cumsum(needed, axis=1) - needed
    chosen = (needed[:, None, :] == 1) & (rank[:, None, :] == jnp.arange(cap)[None, :, None])
    request_ids = jnp.sum(chosen.astype(jnp.int32) * jnp.arange(blocks)[None, None, :], axis=2)
    asked_ids = lax.all_to_all(request_ids, "tile", split_axis=0, concat_axis=0, tiled=True)
    picked_rank = jnp.sum(jnp.where(matches, rank[None], 0), axis=(1, 2))
    slot_index = flat_owner * cap + picked_rank
    slots = peers * cap

    rows = channels + 16
    one = lambda b, *_: (b, 0, 0)
    stored, sums, message = pl.pallas_call(
        atom_kernel,
        grid_spec=pltpu.PrefetchScalarGridSpec(
            num_scalar_prefetch=1,
            grid=(blocks,),
            in_specs=[
                whole(around_feat),
                whole(around_where),
                pl.BlockSpec((1, channels, width), one),
                pl.BlockSpec((1, 16, width), one),
                whole(atom_filter),
            ],
            out_specs=[
                pl.BlockSpec((1, rows, width), one),
                pl.BlockSpec((1, filters * channels, width), one),
                pl.BlockSpec((1, channels, width), one),
            ],
            scratch_shapes=[
                pltpu.VMEM((nbrs * width, 8), F32),
                pltpu.VMEM((nbrs * width, filters * width), BF16),
                pltpu.VMEM((channels, nbrs * width), BF16),
            ],
        ),
        out_shape=[
            jax.ShapeDtypeStruct((blocks, rows, width), BF16),
            jax.ShapeDtypeStruct((blocks, filters * channels, width), BF16),
            jax.ShapeDtypeStruct((blocks, channels, width), F32),
        ],
        compiler_params=params,
        name="atom_layer",
    )(source_rows, around_feat, around_where, atom_feat, where, atom_filter)

    sent = jnp.take(stored, asked_ids.reshape(-1), axis=0).reshape(peers, cap, rows, width)
    replies = lax.all_to_all(sent, "tile", split_axis=0, concat_axis=0, tiled=True)
    replies = replies.reshape(slots, rows, width)

    readout_row = readout.reshape(1, channels)
    density, grad_filter, grad_mix, grad_readout, slot_grad = pl.pallas_call(
        probe_kernel,
        grid_spec=pltpu.PrefetchScalarGridSpec(
            num_scalar_prefetch=1,
            grid=(tiles,),
            in_specs=[
                whole(replies),
                pl.BlockSpec((1, 3, probes), one),
                pl.BlockSpec((1, 1, probes), one),
                whole(probe_filter),
                whole(mix_weight),
                whole(readout_row),
            ],
            out_specs=[
                pl.BlockSpec((1, 1, probes), one),
                pl.BlockSpec((channels, filters * channels), lambda *_: (0, 0)),
                pl.BlockSpec((channels, channels), lambda *_: (0, 0)),
                pl.BlockSpec((8, channels), lambda *_: (0, 0)),
                pl.BlockSpec((slots, channels, width), lambda *_: (0, 0, 0)),
            ],
            scratch_shapes=[
                pltpu.VMEM((reads * width, 8), F32),
                pltpu.VMEM((reads * width, filters * probes), BF16),
                pltpu.VMEM((channels, reads * width), BF16),
                pltpu.VMEM((filters * channels, probes), BF16),
                pltpu.VMEM((filters * probes, channels), BF16),
                pltpu.VMEM((slots, channels, width), F32),
            ],
        ),
        out_shape=[
            jax.ShapeDtypeStruct((tiles, 1, probes), F32),
            jax.ShapeDtypeStruct((channels, filters * channels), F32),
            jax.ShapeDtypeStruct((channels, channels), F32),
            jax.ShapeDtypeStruct((8, channels), F32),
            jax.ShapeDtypeStruct((slots, channels, width), BF16),
        ],
        compiler_params=params,
        name="probe_layer",
    )(
        slot_index, replies, probe_pos, probe_target.reshape(tiles, 1, probes),
        probe_filter, mix_weight, readout_row,
    )

    returned = lax.all_to_all(
        slot_grad.reshape(peers, cap, channels, width), "tile",
        split_axis=0, concat_axis=0, tiled=True,
    ).reshape(slots, channels, width)
    grad_atom = pl.pallas_call(
        final_kernel,
        grid_spec=pltpu.PrefetchScalarGridSpec(
            num_scalar_prefetch=1,
            grid=(blocks,),
            in_specs=[
                whole(returned),
                pl.BlockSpec((1, 16, width), one),
                pl.BlockSpec((1, channels, width), one),
                pl.BlockSpec((1, filters * channels, width), one),
            ],
            out_specs=pl.BlockSpec((channels, filters * channels), lambda *_: (0, 0)),
            scratch_shapes=[pltpu.VMEM((blocks, channels, width), F32)],
        ),
        out_shape=jax.ShapeDtypeStruct((channels, filters * channels), F32),
        compiler_params=params,
        name="atom_grad",
    )(asked_ids.reshape(-1), returned, where, message, sums)

    axes = (("space", space_count), ("tile", peers))
    devices = space_count * peers
    real = 2 * filters * channels + channels + 16
    total_rows = -(-real // (16 * devices)) * 16 * devices
    steps = (devices - 1).bit_length()
    grads = (grad_atom, grad_filter, grad_mix, grad_readout)
    vmem = pl.BlockSpec(memory_space=pltpu.VMEM)
    grad_atom, grad_filter, grad_mix, grad_readout = pl.pallas_call(
        functools.partial(reduce_kernel, axes),
        in_specs=[vmem] * 4,
        out_specs=[vmem] * 4,
        out_shape=[jax.ShapeDtypeStruct(g.shape, F32) for g in grads],
        scratch_shapes=[
            pltpu.VMEM((total_rows, channels), F32),
            pltpu.VMEM((total_rows, channels), BF16),
            pltpu.VMEM((total_rows, channels), BF16),
            pltpu.VMEM((total_rows, channels), BF16),
            pltpu.SemaphoreType.DMA((2 * steps,)),
            pltpu.SemaphoreType.DMA((2 * steps,)),
        ],
        compiler_params=pltpu.CompilerParams(
            vmem_limit_bytes=VMEM_LIMIT, collective_id=0, has_side_effects=True
        ),
        name="grad_reduce",
    )(*grads)
    return (density.reshape(tiles, probes), grad_atom, grad_filter, grad_mix, grad_readout[0])


def solution(mesh):
    return jax.shard_map(
        body,
        mesh=mesh,
        in_specs=(
            P(("space", "tile"), None, None),
            P(("space", "tile"), None, None),
            P(("space", "tile")),
            P(("space", "tile"), None),
            P(("space", "tile"), None, None),
            P(("space", "tile"), None),
            P(("space", "tile"), None),
            P(),
            P(),
            P(),
            P(),
        ),
        out_specs=(P(("space", "tile"), None), P(), P(), P(), P()),
        check_vma=False,
    )
```

time: 436 us -> 210 us (0.48)
  Pallas kernels: 0 us -> 114 us
  waiting for transfers between devices: 145 us -> 52.8 us
  local copies, waits for them, and re-layouts: 105 us -> 13.9 us
  matrix products: 55.9 us -> 0 us
  blocking collectives: 39.6 us -> 0 us
  other arithmetic: 47.9 us -> 8.81 us
  between operations: 14.4 us -> 0.78 us
  loops' own time: 6.15 us -> 0 us
    pallas_call x0 -> x4, Pallas kernels: none -> 114 us  [the longest x1 37 us: body(): pl.pallas_call(functools.partial(reduce_kernel, axes), in_specs=[vmem] *...]
    psum x1 -> x0, waiting for transfers between devices: 93.5 us -> none  [body(): lax.psum((grad_atom, jnp.sum(grad_probe, axis=0), jnp.sum(grad_mix, axis=...]
    dynamic_update_slice x84 -> x0, local copies, waits for them, and re-layouts: 62.3 us -> none  [the longest x80 62.2 us: body(): lax.map(atom_block, (neighbour_rows, atom_pos, atom_feat, atom_mask))]
    dot_general x55 -> x0, matrix products: 55.9 us -> none  [the longest x2 14 us: probe_tile(): jnp.einsum('rcp,krap->kca', grad_summed, kernels, preferred_element_type=...]
    psum x1 -> x0, blocking collectives: 39.6 us -> none  [body(): lax.psum((grad_atom, jnp.sum(grad_probe, axis=0), jnp.sum(grad_mix, axis=...]
    sqrt x18 -> x0, other arithmetic: 34.7 us -> none  [radial(): distance = jnp.sqrt(square + 0.01)]
    dynamic_slice x36 -> x0, local copies, waits for them, and re-layouts: 16.7 us -> none  [the longest x32 14 us: body(): lax.map(atom_block, (neighbour_rows, atom_pos, atom_feat, atom_mask))]
    another operation x2 -> x0, loops' own time: 6.15 us -> none  [the longest x1 4.73 us: body(): lax.map(probe_tile, jnp.arange(tiles_dev))]
  transfers between devices with their start and end apart: 6 -> 7, of which waited for: 4 -> 3; matrix products, arithmetic and copies ran while one was open for 1% -> 4% of each run, Pallas kernels for 0% -> 0%
where the time goes in v1:
time: 210 us; the launch traced here: 209 us
  Pallas kernels  114 us (54%)
  waiting for transfers between devices  52.8 us (25%)
  starting transfers between devices  18.8 us (9%)
  local copies, waits for them, and re-layouts  13.9 us (7%)
  other arithmetic  8.81 us (4%)
    pallas_call x1, Pallas kernels, body(): pl.pallas_call(functools.partial(reduce_kernel, axes), in_specs=[vmem] *...  37 us
    pallas_call x1, Pallas kernels, body(): pl.pallas_call(atom_kernel, grid_spec=pltpu.PrefetchScalarGridSpec(num_sc...  33.7 us
    pallas_call x1, Pallas kernels, body(): pl.pallas_call(probe_kernel, grid_spec=pltpu.PrefetchScalarGridSpec(num_s...  31 us
    all_to_all x1, waiting for transfers between devices, body(): lax.all_to_all(sent, 'tile', split_axis=0, concat_axis=0, tiled=True)  24.9 us
    all_to_all x1, waiting for transfers between devices, body(): lax.all_to_all(slot_grad.reshape(peers, cap, channels, width), 'tile', sp...  23.9 us
    pallas_call x1, Pallas kernels, body(): pl.pallas_call(final_kernel, grid_spec=pltpu.PrefetchScalarGridSpec(num_s...  12.7 us
    unnamed x22, local copies, waits for them, and re-layouts  7.31 us
    all_to_all x1, starting transfers between devices, body(): lax.all_to_all(request_ids, 'tile', split_axis=0, concat_axis=0, tiled=True)  5.56 us
  transfers between devices with their start and end apart: 7, of which 3 were waited for; matrix products, arithmetic and copies ran while one was open for 4% of the time, Pallas kernels for 0%

profile of v1, /device:TPU:1, one launch (start us, length us, event | category | flops | bytes accessed | tf_op | source)
XLA Modules:
  0.0 209.5 jit_solution(3356809541962652650)
XLA Ops:
  0.6 0.7 compare_convert_fusion
  1.4 0.7 copy.38
  2.2 2.6 %collective-permute-start.2 = (bf16[16,16,128]{2,1,0:T(8,128)(2,1)S(1)}, bf16[16,16,128]{2,1,0:T(8,128)(2,1)S(1)}, u32[]{:S(2)}, u32[]{:S(2)}) collective-permute-start(bf16[16,16,128]{2,1,0:T(8,128)(2,1)S(1)} %pad_maximum_fusion.2.own_where_ref.where_ref), channel_id=1, source_target_pairs={{0,8},{8,16},{16,24},{24,0},{1,9},{9,17},{17,25},{25,1},{2,10},{10... | collective-permute-start | bytes 196616 | tf_op jit(solution)/shard_map/ppermute | solution.py:317
  4.9 1.7 collective-permute-start
  6.6 0.7 and_select_fusion.2
  8.1 0.7 copy.34
  8.8 5.6 %all-to-all-start = ((s32[8,1,4]{2,1,0:T(1,128)}), s32[8,1,4]{2,1,0:T(1,128)S(1)}, u32[]{:S(2)}, u32[]{:S(2)}) async-start(s32[8,1,4]{2,1,0:T(1,128)} %copy.34), calls=%async_computation | async-start | bytes 8192 | tf_op jit(solution)/shard_map/all_to_all | solution.py:336
  14.3 0.7 fusion.7
  15.1 0.6 reshape.185.rows_ref
  15.7 3.9 %all-to-all-done = s32[8,1,4]{2,1,0:T(1,128)S(1)} async-done(((s32[8,1,4]{2,1,0:T(1,128)}), s32[8,1,4]{2,1,0:T(1,128)S(1)}, u32[]{:S(2)}, u32[]{:S(2)}) %all-to-all-start) | async-done | bytes 160 | tf_op jit(solution)/shard_map/all_to_all | solution.py:336
  20.2 0.7 reduce.5
  21.1 0.7 pad_maximum_fusion.1.where_ref
  21.8 2.4 %pad_maximum_fusion.around_ref = bf16[48,128,128]{2,1,0:T(8,128)(2,1)} fusion(bf16[16,128,128]{2,1,0:T(8,128)(2,1)S(1)} %collective-permute-done.1, bf16[16,128,128]{2,1,0:T(8,128)(2,1)} %own_feat_ref.1, bf16[16,128,128]{2,1,0:T(8,128)(2,1)S(1)} %collective-permute-done), kind=kLoop, calls=%fused_computation.1 | loop fusion | flops 1572864 | bytes 3145728 | tf_op jit(solution)/shard_map/concatenate | solution.py:307
  24.2 33.7 %atom_layer.1 = (bf16[16,144,128]{2,1,0:T(8,128)(2,1)}, bf16[16,1024,128]{2,1,0:T(8,128)(2,1)}, f32[16,128,128]{2,1,0:T(8,128)}) custom-call(s32[64]{0:T(128)} %reshape.185.rows_ref, bf16[48,128,128]{2,1,0:T(8,128)(2,1)} %pad_maximum_fusion.around_ref, bf16[48,16,128]{2,1,0:T(8,128)(2,1)} %pad_maximum_fusion.1.where_ref, bf16[16,128,128]{2,1,0:T(8,128)(2,1)} %own_feat_ref.1, ...), custom_call_target="tpu_custom_call" | custom-call | tf_op jit(solution)/shard_map/atom_layer/pallas_call | solution.py:343
  57.9 1.8 gather_fusion
  59.8 1.2 broadcast_select_fusion
  61.0 3.7 %all-to-all-start.1 = ((bf16[8,4,144,128]{3,2,1,0:T(8,128)(2,1)}), bf16[8,4,144,128]{3,2,1,0:T(8,128)(2,1)S(1)}, u32[]{:S(2)}, u32[]{:S(2)}) async-start(bf16[8,4,144,128]{3,2,1,0:T(8,128)(2,1)} %broadcast_select_fusion), calls=%async_computation.1 | async-start | bytes 2359296 | tf_op jit(solution)/shard_map/all_to_all | solution.py:376
  64.8 0.6 reshape.188.target_ref
  65.4 0.6 copy.39.where_ref
  66.9 24.9 %all-to-all-done.1 = bf16[8,4,144,128]{3,2,1,0:T(8,128)(2,1)S(1)} async-done(((bf16[8,4,144,128]{3,2,1,0:T(8,128)(2,1)}), bf16[8,4,144,128]{3,2,1,0:T(8,128)(2,1)S(1)}, u32[]{:S(2)}, u32[]{:S(2)}) %all-to-all-start.1) | async-done | bytes 1179680 | tf_op jit(solution)/shard_map/all_to_all | solution.py:376
  91.9 1.1 copy-done
  92.9 31.0 %probe_layer.1 = (f32[2,1,512]{2,1,0:T(1,128)}, f32[128,1024]{1,0:T(8,128)}, f32[128,128]{1,0:T(8,128)}, f32[8,128]{1,0:T(8,128)}, bf16[32,128,128]{2,1,0:T(8,128)(2,1)}) custom-call(s32[16]{0:T(128)} %multiply_add_fusion.slots_ref, bf16[32,144,128]{2,1,0:T(8,128)(2,1)} %bitcast.19, f32[2,3,512]{2,1,0:T(4,128)} %copy.39.where_ref, ...), custom_call_target="tpu_custom_call" | custom-call | tf_op jit(solution)/shard_map/probe_layer/pallas_call | solution.py:380
  124.0 5.1 %all-to-all-start.2 = ((bf16[8,4,128,128]{3,2,1,0:T(8,128)(2,1)}), bf16[8,4,128,128]{3,2,1,0:T(8,128)(2,1)S(1)}, u32[]{:S(2)}, u32[]{:S(2)}) async-start(bf16[8,4,128,128]{3,2,1,0:T(8,128)(2,1)} %bitcast.21), calls=%async_computation.2 | async-start | bytes 2097152 | tf_op jit(solution)/shard_map/all_to_all | solution.py:423
  129.7 0.6 copy.42
  130.3 23.9 %all-to-all-done.2 = bf16[8,4,128,128]{3,2,1,0:T(8,128)(2,1)S(1)} async-done(((bf16[8,4,128,128]{3,2,1,0:T(8,128)(2,1)}), bf16[8,4,128,128]{3,2,1,0:T(8,128)(2,1)S(1)}, u32[]{:S(2)}, u32[]{:S(2)}) %all-to-all-start.2) | async-done | bytes 1048608 | tf_op jit(solution)/shard_map/all_to_all | solution.py:423
  154.2 1.0 copy-done.1
  155.2 12.7 %atom_grad.1.atom_ref = f32[128,1024]{1,0:T(8,128)} custom-call(s32[32]{0:T(128)} %reshape.191.ids_ref, bf16[32,128,128]{2,1,0:T(8,128)(2,1)} %bitcast.20, bf16[16,16,128]{2,1,0:T(8,128)(2,1)} %copy-done.2, f32[16,128,128]{2,1,0:T(8,128)} %get-tuple-element.20.message_ref, bf16[16,1024,128]{2,1,0:T(8,128)(2,1)} %get-tuple-element.21.sums_ref), custom_call_target="tpu_custom_call" | custom-call | tf_op jit(solution)/shard_map/atom_grad/pallas_call | solution.py:427
  167.9 37.0 %grad_reduce.1 = (f32[128,1024]{1,0:T(8,128)}, f32[128,1024]{1,0:T(8,128)}, f32[128,128]{1,0:T(8,128)}, f32[8,128]{1,0:T(8,128)}) custom-call(f32[128,1024]{1,0:T(8,128)} %atom_grad.1.atom_ref, f32[128,1024]{1,0:T(8,128)} %get-tuple-element.22.filter_ref, f32[128,128]{1,0:T(8,128)} %get-tuple-element.23.mix_ref, f32[8,128]{1,0:T(8,128)} %get-tuple-element.24.readout_ref), custom_call_target="tpu_custom_call" | custom-call | tf_op jit(solution)/shard_map/grad_reduce/pallas_call | solution.py:453
  204.9 1.2 slice_bitcast_fusion
  206.2 1.9 copy.46
  208.1 0.8 copy.47
  208.9 0.6 copy.48
  (42 shorter events, 3.3 us)
Async XLA Ops:
  2.2 22.1 %copy-start.2 = (bf16[16,16,128]{2,1,0:T(8,128)(2,1)}, bf16[16,16,128]{2,1,0:T(8,128)(2,1)S(1)}, u32[]{:S(2)}) copy-start(bf16[16,16,128]{2,1,0:T(8,128)(2,1)S(1)} %pad_maximum_fusion.2.own_where_ref.where_ref) | copy-start | bytes 196612
  2.2 18.9 %collective-permute-start.3 = (bf16[16,16,128]{2,1,0:T(8,128)(2,1)S(1)}, bf16[16,16,128]{2,1,0:T(8,128)(2,1)S(1)}, u32[]{:S(2)}, u32[]{:S(2)}) collective-permute-start(bf16[16,16,128]{2,1,0:T(8,128)(2,1)S(1)} %pad_maximum_fusion.2.own_where_ref.where_ref), channel_id=1, source_target_pairs={{8,0},{16,8},{24,16},{0,24},{9,1},{17,9},{25,17},{1,25},{10,2},{18... | collective-permute-start | bytes 196616 | tf_op jit(solution)/shard_map/ppermute | solution.py:319
  2.2 18.8 %collective-permute-start.2 = (bf16[16,16,128]{2,1,0:T(8,128)(2,1)S(1)}, bf16[16,16,128]{2,1,0:T(8,128)(2,1)S(1)}, u32[]{:S(2)}, u32[]{:S(2)}) collective-permute-start(bf16[16,16,128]{2,1,0:T(8,128)(2,1)S(1)} %pad_maximum_fusion.2.own_where_ref.where_ref), channel_id=1, source_target_pairs={{0,8},{8,16},{16,24},{24,0},{1,9},{9,17},{17,25},{25,1},{2,10},{10... | collective-permute-start | bytes 196616 | tf_op jit(solution)/shard_map/ppermute | solution.py:317
  4.9 16.9 %collective-permute-start.1 = (bf16[16,128,128]{2,1,0:T(8,128)(2,1)}, bf16[16,128,128]{2,1,0:T(8,128)(2,1)S(1)}, u32[]{:S(2)}, u32[]{:S(2)}) collective-permute-start(bf16[16,128,128]{2,1,0:T(8,128)(2,1)} %own_feat_ref.1), channel_id=1, source_target_pairs={{8,0},{16,8},{24,16},{0,24},{9,1},{17,9},{25,17},{1,25},{10,2},{18... | collective-permute-start | bytes 1572872 | tf_op jit(solution)/shard_map/ppermute | solution.py:311
  4.9 16.9 %collective-permute-start = (bf16[16,128,128]{2,1,0:T(8,128)(2,1)}, bf16[16,128,128]{2,1,0:T(8,128)(2,1)S(1)}, u32[]{:S(2)}, u32[]{:S(2)}) collective-permute-start(bf16[16,128,128]{2,1,0:T(8,128)(2,1)} %own_feat_ref.1), channel_id=1, source_target_pairs={{0,8},{8,16},{16,24},{24,0},{1,9},{9,17},{17,25},{25,1},{2,10},{10... | collective-permute-start | bytes 1572872 | tf_op jit(solution)/shard_map/ppermute | solution.py:309
  8.8 10.8 %all-to-all-start = ((s32[8,1,4]{2,1,0:T(1,128)}), s32[8,1,4]{2,1,0:T(1,128)S(1)}, u32[]{:S(2)}, u32[]{:S(2)}) async-start(s32[8,1,4]{2,1,0:T(1,128)} %copy.34), calls=%async_computation | async-start | bytes 8192 | tf_op jit(solution)/shard_map/all_to_all | solution.py:336
  61.0 3.7 %copy-start.6 = (f32[2,512]{1,0:T(2,128)S(1)}, f32[2,512]{1,0:T(2,128)}, u32[]{:S(2)}) copy-start(f32[2,512]{1,0:T(2,128)} %param.16) | copy-start | bytes 12292
  61.0 4.3 %copy-start.5 = (f32[2,3,512]{2,0,1:T(2,128)S(1)}, f32[2,3,512]{2,0,1:T(2,128)}, u32[]{:S(2)}) copy-start(f32[2,3,512]{2,0,1:T(2,128)} %param.15) | copy-start | bytes 36868
  61.0 30.8 %all-to-all-start.1 = ((bf16[8,4,144,128]{3,2,1,0:T(8,128)(2,1)}), bf16[8,4,144,128]{3,2,1,0:T(8,128)(2,1)S(1)}, u32[]{:S(2)}, u32[]{:S(2)}) async-start(bf16[8,4,144,128]{3,2,1,0:T(8,128)(2,1)} %broadcast_select_fusion), calls=%async_computation.1 | async-start | bytes 2359296 | tf_op jit(solution)/shard_map/all_to_all | solution.py:376
  91.9 1.1 copy-start
  124.0 5.7 %copy-start.7 = (f32[2,1,512]{2,1,0:T(1,128)S(1)}, f32[2,1,512]{2,1,0:T(1,128)}, u32[]{:S(2)}) copy-start(f32[2,1,512]{2,1,0:T(1,128)} %get-tuple-element.18) | copy-start | bytes 12292
  124.0 30.3 %all-to-all-start.2 = ((bf16[8,4,128,128]{3,2,1,0:T(8,128)(2,1)}), bf16[8,4,128,128]{3,2,1,0:T(8,128)(2,1)S(1)}, u32[]{:S(2)}, u32[]{:S(2)}) async-start(bf16[8,4,128,128]{3,2,1,0:T(8,128)(2,1)} %bitcast.21), calls=%async_computation.2 | async-start | bytes 2097152 | tf_op jit(solution)/shard_map/all_to_all | solution.py:423
  154.2 1.0 copy-start.1
  204.9 3.1 %copy-start.3 = (f32[128,1024]{1,0:T(8,128)S(1)}, f32[128,1024]{1,0:T(8,128)}, u32[]{:S(2)}) copy-start(f32[128,1024]{1,0:T(8,128)} %get-tuple-element.40) | copy-start | bytes 1572868
  204.9 3.9 %copy-start.4 = (f32[128,128]{1,0:T(8,128)S(1)}, f32[128,128]{1,0:T(8,128)}, u32[]{:S(2)}) copy-start(f32[128,128]{1,0:T(8,128)} %get-tuple-element.41) | copy-start | bytes 196612

commit v2 on v1

v2 whole, which is shorter than its diff:
```python
import functools
import math

import jax
import jax.numpy as jnp
from jax import lax
from jax.experimental import pallas as pl
from jax.experimental.pallas import tpu as pltpu
from jax.sharding import PartitionSpec as P

CUTOFF = 6.0
SPACING = 0.75
SPREAD = 0.75
LOG2E = 1.4426950408889634
MESH = pl.DeviceIdType.MESH
VMEM_LIMIT = 56 * 1024 * 1024
F32 = jnp.float32
BF16 = jnp.bfloat16


def silu_slope(values):
    s = jax.nn.sigmoid(values)
    return s * (1.0 + values * (1.0 - s))


def radial(source_cols, target_rows, factor, filters, keep=None):
    square = None
    for source, target in zip(source_cols, target_rows):
        offset = source - target
        square = offset * offset if square is None else square + offset * offset
    square = square + 0.01
    distance = square * lax.rsqrt(square)
    half = (math.pi / (2.0 * CUTOFF)) ** 2
    terms = [math.sqrt(factor) * (-half) ** k / math.factorial(2 * k) for k in range(7)]
    wave = terms[6] * square + terms[5]
    for term in terms[4::-1]:
        wave = wave * square + term
    envelope = jnp.where(square < CUTOFF * CUTOFF, wave * wave, 0.0)
    middle = filters // 2
    shifted = distance * (1.0 / SPREAD) - middle * (SPACING / SPREAD)
    step = SPACING / SPREAD
    centre = envelope * jnp.exp2(shifted * shifted * (-LOG2E))
    if keep is not None:
        centre = centre * keep
    ratio = 2.0 * step * LOG2E
    up = jnp.exp2(shifted * ratio - step * step * LOG2E)
    down = jnp.exp2(shifted * (-ratio) - step * step * LOG2E)
    values = [None] * filters
    values[middle] = centre
    now = centre
    for k in range(filters - 1 - middle):
        now = now * (up if k == 0 else up * math.exp(-2.0 * k * step * step))
        values[middle + k + 1] = now
    now = centre
    for k in range(middle):
        now = now * (down if k == 0 else down * math.exp(-2.0 * k * step * step))
        values[middle - k - 1] = now
    return values


def dot(a, b):
    return jnp.dot(a, b, preferred_element_type=F32)


def dot_nt(a, b):
    return lax.dot_general(a, b, (((1,), (1,)), ((), ())), preferred_element_type=F32)


def atom_radial_kernel(rows_ref, around_where_ref, own_where_ref, radial_ref, columns):
    block = pl.program_id(0)
    width = own_where_ref.shape[2]
    nbrs = radial_ref.shape[1] // width
    filters = radial_ref.shape[2] // width
    factor = (nbrs * width) ** (-0.5)
    own = own_where_ref[0].astype(F32)
    target = [own[c : c + 1, :] for c in range(3)]
    for k in range(nbrs):
        where = around_where_ref[rows_ref[block * nbrs + k]].astype(F32)
        columns[k * width : (k + 1) * width, :] = where[:8].T
    chunk = 32

    def fill(step, carry):
        start = pl.multiple_of(step * chunk, chunk)
        source = [columns[pl.ds(start, chunk), c : c + 1] for c in range(3)]
        keep = columns[pl.ds(start, chunk), 3:4]
        for r, value in enumerate(radial(source, target, factor, filters, keep)):
            radial_ref[0, pl.ds(start, chunk), r * width : (r + 1) * width] = value.astype(BF16)
        return carry

    lax.fori_loop(0, nbrs * width // chunk, fill, 0, unroll=2)


def atom_kernel(
    rows_ref, sides_ref, asked_ref, low_ref, own_ref, high_ref, radial_ref, where_ref, filter_ref,
    sent_ref, sums_ref, message_ref, feats, updated,
):
    block = pl.program_id(0)
    channels, width = own_ref.shape[1:]
    filters = filter_ref.shape[1] // channels
    nbrs = feats.shape[1] // width
    for k in range(nbrs):
        row = rows_ref[block * nbrs + k]
        part = (slice(None), slice(k * width, (k + 1) * width))
        if k < 3:
            feats[part] = (low_ref, high_ref, own_ref)[k][row]
            continue
        side = sides_ref[block * nbrs + k]
        for n, ref in enumerate((low_ref, own_ref, high_ref)):

            @pl.when(side == n)
            def _(ref=ref, row=row, part=part):
                feats[part] = ref[row]

    total = dot(feats[...], radial_ref[0]).astype(BF16)
    for r in range(filters):
        sums_ref[0, r * channels : (r + 1) * channels, :] = total[:, r * width : (r + 1) * width]
    message = dot(filter_ref[...], sums_ref[0])
    message_ref[0] = message
    keep = where_ref[0].astype(F32)[3:4, :]
    fresh = (own_ref[block].astype(F32) + message * jax.nn.sigmoid(message)) * keep
    updated[block] = fresh.astype(BF16)

    @pl.when(block == pl.num_programs(0) - 1)
    def _():
        def pick(slot, carry):
            sent_ref[slot] = updated[asked_ref[slot]]
            return carry

        lax.fori_loop(0, sent_ref.shape[0], pick, 0)


def probe_radial_kernel(source_ref, where_ref, radial_ref, columns):
    width = source_ref.shape[2]
    reads = source_ref.shape[0]
    probes = where_ref.shape[2]
    filters = radial_ref.shape[2] // probes
    factor = (pl.num_programs(1) * reads * width) ** (-0.5)
    for k in range(reads):
        columns[k * width : (k + 1) * width, :] = source_ref[k].T
    chunk, span = 16, 256
    lanes = []
    for p in range(0, probes, span):
        lanes.append([where_ref[0, c : c + 1, p : p + span] for c in range(3)])

    def fill(step, carry):
        start = pl.multiple_of(step * chunk, chunk)
        source = [columns[pl.ds(start, chunk), c : c + 1] for c in range(3)]
        for n, target in enumerate(lanes):
            for r, value in enumerate(radial(source, target, factor, filters)):
                low = r * probes + n * span
                radial_ref[0, pl.ds(start, chunk), low : low + span] = value.astype(BF16)
        return carry

    lax.fori_loop(0, reads * width // chunk, fill, 0)


def probe_kernel(
    slots_ref, replies_ref, radial_ref, target_ref, filter_ref, mix_ref, readout_ref,
    density_ref, grad_filter_ref, grad_mix_ref, grad_readout_ref, slot_grad_ref,
    feats, summed, turned, slot_total,
):
    tile = pl.program_id(0)
    tiles = pl.num_programs(0)
    channels = mix_ref.shape[0]
    filters = filter_ref.shape[1] // channels
    width = replies_ref.shape[2]
    reads = feats.shape[1] // width
    probes = target_ref.shape[2]

    @pl.when(tile == 0)
    def _():
        slot_total[...] = jnp.zeros_like(slot_total)
        grad_filter_ref[...] = jnp.zeros_like(grad_filter_ref)
        grad_mix_ref[...] = jnp.zeros_like(grad_mix_ref)
        grad_readout_ref[...] = jnp.zeros_like(grad_readout_ref)

    for k in range(reads):
        feats[:, k * width : (k + 1) * width] = replies_ref[slots_ref[tile * reads + k]]
    for r in range(filters):
        summed[r * channels : (r + 1) * channels, :] = dot(
            feats[...], radial_ref[0, :, r * probes : (r + 1) * probes]
        ).astype(BF16)
    hidden = dot(filter_ref[...], summed[...])
    gate = jax.nn.sigmoid(hidden)
    squashed = (hidden * gate).astype(BF16)
    mixed = dot(mix_ref[...], squashed)
    mixed_gate = jax.nn.sigmoid(mixed)
    outer = mixed * mixed_gate
    readout = jnp.broadcast_to(readout_ref[...], (8, channels)).T[:, :1]
    density = jnp.sum(readout * outer, axis=0, keepdims=True)
    density_ref[0] = density
    misfit = (density - target_ref[0]) / probes
    part = jnp.sum(outer * misfit, axis=1, keepdims=True)
    grad_readout_ref[...] += jnp.broadcast_to(part, (channels, channels)).T[:8, :]
    grad_mixed = (
        readout * misfit * (mixed_gate * (1.0 + mixed * (1.0 - mixed_gate)))
    ).astype(BF16)
    grad_mix_ref[...] += dot_nt(grad_mixed, squashed)
    grad_squashed = dot(mix_ref[...].T, grad_mixed)
    grad_hidden = (grad_squashed * (gate * (1.0 + hidden * (1.0 - gate)))).astype(BF16)
    grad_filter_ref[...] += dot_nt(grad_hidden, summed[...])
    grad_sums = dot(grad_hidden.T, filter_ref[...]).astype(BF16)
    for r in range(filters):
        turned[r * probes : (r + 1) * probes, :] = grad_sums[:, r * channels : (r + 1) * channels]
    for k in range(reads):
        slot = slots_ref[tile * reads + k]
        back = dot(radial_ref[0, k * width : (k + 1) * width, :], turned[...])
        slot_total[slot] += back.T

    @pl.when(tile == tiles - 1)
    def _():
        slot_grad_ref[...] = slot_total[...].astype(BF16)


def final_kernel(ids_ref, returned_ref, where_ref, message_ref, sums_ref, grad_ref, totals):
    step = pl.program_id(0)
    group = sums_ref.shape[0]

    @pl.when(step == 0)
    def _():
        totals[...] = jnp.zeros_like(totals)

        def add(slot, carry):
            totals[ids_ref[slot]] += returned_ref[slot].astype(F32)
            return carry

        lax.fori_loop(0, returned_ref.shape[0], add, 0)

    grads = []
    for n in range(group):
        keep = where_ref[n].astype(F32)[3:4, :]
        grad = totals[step * group + n] * keep * silu_slope(message_ref[n])
        grads.append(grad.astype(BF16))
    part = dot_nt(
        jnp.concatenate(grads, axis=1),
        jnp.concatenate([sums_ref[n] for n in range(group)], axis=1),
    )

    @pl.when(step == 0)
    def _():
        grad_ref[...] = part

    @pl.when(step > 0)
    def _():
        grad_ref[...] += part


def reduce_kernel(axes, count, *refs):
    ins, outs = refs[:count], refs[count : 2 * count]
    total, sending, landing, gathered, send_sems, recv_sems = refs[2 * count :]
    lanes = total.shape[1]
    rows = total.shape[0]
    partners = []
    for axis, size in axes:
        here = lax.axis_index(axis)
        bit = 1
        while bit < size:
            side = (here // bit) % 2
            partners.append((axis, here + bit * (1 - 2 * side), side))
            bit *= 2
    barrier = pltpu.get_barrier_semaphore()
    for axis, other, _ in partners:
        pl.semaphore_signal(barrier, inc=1, device_id={axis: other}, device_id_type=MESH)
    pieces = []
    low = 0
    for index, ref in enumerate(ins):
        height = ref.shape[0]
        for left in range(0, ref.shape[1], lanes):
            total[low : low + height, :] = ref[:, left : left + lanes]
            pieces.append((index, left, low, height))
            low += height
    if low < rows:
        total[low:, :] = jnp.zeros((rows - low, lanes), F32)
    pl.semaphore_wait(barrier, len(partners))
    start = 0
    size = rows
    place = 0
    copies = []
    ranges = []
    for n, (axis, other, side) in enumerate(partners):
        size //= 2
        keep = pl.multiple_of(start + side * size, 16)
        give = pl.multiple_of(start + (1 - side) * size, 16)
        sending[place : place + size, :] = total[pl.ds(give, size), :].astype(BF16)
        copy = pltpu.make_async_remote_copy(
            src_ref=sending.at[pl.ds(place, size)],
            dst_ref=landing.at[pl.ds(place, size)],
            send_sem=send_sems.at[n],
            recv_sem=recv_sems.at[n],
            device_id={axis: other},
            device_id_type=MESH,
        )
        copy.start()
        copy.wait_recv()
        total[pl.ds(keep, size), :] += landing[place : place + size, :].astype(F32)
        copies.append(copy)
        ranges.append((keep, size))
        place += size
        start = keep
    keep, size = ranges[-1]
    gathered[pl.ds(keep, size), :] = total[pl.ds(keep, size), :].astype(BF16)
    for n in range(len(partners) - 1, -1, -1):
        axis, other, _ = partners[n]
        keep, size = ranges[n]
        copy = pltpu.make_async_remote_copy(
            src_ref=gathered.at[pl.ds(keep, size)],
            dst_ref=gathered.at[pl.ds(keep, size)],
            send_sem=send_sems.at[len(partners) + n],
            recv_sem=recv_sems.at[len(partners) + n],
            device_id={axis: other},
            device_id_type=MESH,
        )
        copy.start()
        copy.wait_recv()
        copies.append(copy)
    for index, left, low, height in pieces:
        padded = -(-height // 16) * 16
        part = gathered[low : low + padded, :].astype(F32)[:height]
        outs[index][:, left : left + lanes] = part
    for copy in copies:
        copy.wait_send()


def reduce_all(grads, axes, name, collective_id):
    devices = math.prod(size for _, size in axes)
    lanes = grads[0].shape[0]
    real = sum(-(-g.size // (16 * lanes)) * 16 for g in grads)
    rows = -(-real // (16 * devices)) * 16 * devices
    steps = (devices - 1).bit_length()
    vmem = pl.BlockSpec(memory_space=pltpu.VMEM)
    return pl.pallas_call(
        functools.partial(reduce_kernel, axes, len(grads)),
        in_specs=[vmem] * len(grads),
        out_specs=[vmem] * len(grads),
        out_shape=[jax.ShapeDtypeStruct(g.shape, F32) for g in grads],
        scratch_shapes=[
            pltpu.VMEM((rows, lanes), F32),
            pltpu.VMEM((rows, lanes), BF16),
            pltpu.VMEM((rows, lanes), BF16),
            pltpu.VMEM((rows, lanes), BF16),
            pltpu.SemaphoreType.DMA((2 * steps,)),
            pltpu.SemaphoreType.DMA((2 * steps,)),
        ],
        compiler_params=pltpu.CompilerParams(
            vmem_limit_bytes=16 * 1024 * 1024, collective_id=collective_id, has_side_effects=True
        ),
        cost_estimate=cost(20e9),
        name=name,
    )(*grads)


def cost(flops):
    return pl.CostEstimate(flops=int(flops), bytes_accessed=1 << 20, transcendentals=0)


def whole(array):
    return pl.BlockSpec(array.shape, lambda *_: (0,) * array.ndim)


def body(
    atom_feat, atom_pos, atom_counts, atom_nbrs, probe_pos, probe_target, tile_blocks,
    atom_filter, probe_filter, mix_weight, readout,
):
    blocks, channels, width = atom_feat.shape
    tiles, reads = tile_blocks.shape
    probes = probe_pos.shape[2]
    filters = atom_filter.shape[1] // channels
    nbrs = atom_nbrs.shape[1]
    peers = lax.axis_size("tile")
    space_count = lax.axis_size("space")
    here = lax.axis_index("space")
    params = pltpu.CompilerParams(vmem_limit_bytes=VMEM_LIMIT)
    small = pltpu.CompilerParams(vmem_limit_bytes=16 * 1024 * 1024)
    mask = (jnp.arange(width)[None, :] < atom_counts[:, None]).astype(BF16)
    where = jnp.concatenate(
        [atom_pos, mask[:, None, :], jnp.zeros((blocks, 12, width), BF16)], axis=1
    )
    forward = [(i, (i + 1) % space_count) for i in range(space_count)]
    backward = [(b, a) for a, b in forward]
    low_feat = lax.ppermute(atom_feat, "space", forward)
    high_feat = lax.ppermute(atom_feat, "space", backward)
    around_where = jnp.concatenate(
        [lax.ppermute(where, "space", forward), where, lax.ppermute(where, "space", backward)],
        axis=0,
    )
    sides = ((atom_nbrs // (peers * blocks) - here + 1) % space_count).reshape(-1)
    near_rows = (atom_nbrs % blocks).reshape(-1)

    flat_owner = (tile_blocks // blocks % peers).reshape(-1)
    flat_spot = (tile_blocks % blocks).reshape(-1)
    cap = max(2, 2 * reads * tiles // peers)
    slots = peers * cap
    matches = (flat_owner[:, None, None] == jnp.arange(peers)[None, :, None]) & (
        flat_spot[:, None, None] == jnp.arange(blocks)[None, None, :]
    )
    needed = jnp.any(matches, axis=0).astype(jnp.int32)
    rank = jnp.cumsum(needed, axis=1) - needed
    chosen = (needed[:, None, :] == 1) & (rank[:, None, :] == jnp.arange(cap)[None, :, None])
    request_ids = jnp.sum(chosen.astype(jnp.int32) * jnp.arange(blocks)[None, None, :], axis=2)
    picked_rank = jnp.sum(jnp.where(matches, rank[None], 0), axis=(1, 2))
    slot_index = flat_owner * cap + picked_rank
    flat_where = jnp.broadcast_to(
        atom_pos.reshape(1, blocks * 3, width), (peers, blocks * 3, width)
    )
    asked_row = jnp.pad(request_ids.astype(BF16)[:, None, :], ((0, 0), (0, 15), (0, width - cap)))
    notes = lax.all_to_all(
        jnp.concatenate([flat_where, asked_row], axis=1), "tile",
        split_axis=0, concat_axis=0, tiled=True,
    )
    asked_ids = notes[:, blocks * 3, :cap].astype(jnp.int32).reshape(-1)
    group_where = notes[:, : blocks * 3, :].reshape(peers * blocks, 3, width)

    one = lambda b, *_: (b, 0, 0)
    atom_radial = pl.pallas_call(
        atom_radial_kernel,
        grid_spec=pltpu.PrefetchScalarGridSpec(
            num_scalar_prefetch=1,
            grid=(blocks,),
            in_specs=[whole(around_where), pl.BlockSpec((1, 16, width), one)],
            out_specs=pl.BlockSpec((1, nbrs * width, filters * width), one),
            scratch_shapes=[pltpu.VMEM((nbrs * width, 8), F32)],
        ),
        out_shape=jax.ShapeDtypeStruct((blocks, nbrs * width, filters * width), BF16),
        compiler_params=small,
        cost_estimate=cost(20e9),
        name="atom_radial",
    )(sides * blocks + near_rows, around_where, where)

    sent, sums, message = pl.pallas_call(
        atom_kernel,
        grid_spec=pltpu.PrefetchScalarGridSpec(
            num_scalar_prefetch=3,
            grid=(blocks,),
            in_specs=[
                whole(low_feat),
                whole(atom_feat),
                whole(high_feat),
                pl.BlockSpec((1, nbrs * width, filters * width), one),
                pl.BlockSpec((1, 16, width), one),
                whole(atom_filter),
            ],
            out_specs=[
                pl.BlockSpec((slots, channels, width), lambda *_: (0, 0, 0)),
                pl.BlockSpec((1, filters * channels, width), one),
                pl.BlockSpec((1, channels, width), one),
            ],
            scratch_shapes=[
                pltpu.VMEM((channels, nbrs * width), BF16),
                pltpu.VMEM((blocks, channels, width), BF16),
            ],
        ),
        out_shape=[
            jax.ShapeDtypeStruct((slots, channels, width), BF16),
            jax.ShapeDtypeStruct((blocks, filters * channels, width), BF16),
            jax.ShapeDtypeStruct((blocks, channels, width), F32),
        ],
        compiler_params=params,
        cost_estimate=cost(10e9),
        name="atom_layer",
    )(near_rows, sides, asked_ids, low_feat, atom_feat, high_feat, atom_radial, where, atom_filter)

    sent, group_where = lax.optimization_barrier((sent, group_where))
    replies = lax.all_to_all(
        sent.reshape(peers, cap, channels, width), "tile",
        split_axis=0, concat_axis=0, tiled=True,
    ).reshape(slots, channels, width)

    source_where = jnp.take(group_where, flat_owner * blocks + flat_spot, axis=0).astype(F32)
    source_where = jnp.pad(source_where, ((0, 0), (0, 5), (0, 0)))
    pieces = reads // 2
    per = reads // pieces
    probe_radial = pl.pallas_call(
        probe_radial_kernel,
        grid=(tiles, pieces),
        in_specs=[
            pl.BlockSpec((per, 8, width), lambda t, n: (t * pieces + n, 0, 0)),
            pl.BlockSpec((1, 3, probes), lambda t, n: (t, 0, 0)),
        ],
        out_specs=pl.BlockSpec((1, per * width, filters * probes), lambda t, n: (t, n, 0)),
        scratch_shapes=[pltpu.VMEM((per * width, 8), F32)],
        out_shape=jax.ShapeDtypeStruct((tiles, reads * width, filters * probes), BF16),
        compiler_params=small,
        cost_estimate=cost(20e9),
        name="probe_radial",
    )(source_where, probe_pos)

    readout_row = readout.reshape(1, channels)
    density, grad_filter, grad_mix, grad_readout, slot_grad = pl.pallas_call(
        probe_kernel,
        grid_spec=pltpu.PrefetchScalarGridSpec(
            num_scalar_prefetch=1,
            grid=(tiles,),
            in_specs=[
                whole(replies),
                pl.BlockSpec((1, reads * width, filters * probes), one),
                pl.BlockSpec((1, 1, probes), one),
                whole(probe_filter),
                whole(mix_weight),
                whole(readout_row),
            ],
            out_specs=[
                pl.BlockSpec((1, 1, probes), one),
                pl.BlockSpec((channels, filters * channels), lambda *_: (0, 0)),
                pl.BlockSpec((channels, channels), lambda *_: (0, 0)),
                pl.BlockSpec((8, channels), lambda *_: (0, 0)),
                pl.BlockSpec((slots, channels, width), lambda *_: (0, 0, 0)),
            ],
            scratch_shapes=[
                pltpu.VMEM((channels, reads * width), BF16),
                pltpu.VMEM((filters * channels, probes), BF16),
                pltpu.VMEM((filters * probes, channels), BF16),
                pltpu.VMEM((slots, channels, width), F32),
            ],
        ),
        out_shape=[
            jax.ShapeDtypeStruct((tiles, 1, probes), F32),
            jax.ShapeDtypeStruct((channels, filters * channels), F32),
            jax.ShapeDtypeStruct((channels, channels), F32),
            jax.ShapeDtypeStruct((8, channels), F32),
            jax.ShapeDtypeStruct((slots, channels, width), BF16),
        ],
        compiler_params=params,
        cost_estimate=cost(10e9),
        name="probe_layer",
    )(
        slot_index, replies, probe_radial, probe_target.reshape(tiles, 1, probes),
        probe_filter, mix_weight, readout_row,
    )

    returned = lax.all_to_all(
        slot_grad.reshape(peers, cap, channels, width), "tile",
        split_axis=0, concat_axis=0, tiled=True,
    ).reshape(slots, channels, width)
    axes = (("space", space_count), ("tile", peers))
    grad_filter, grad_mix, grad_readout = reduce_all(
        (grad_filter, grad_mix, grad_readout), axes, "probe_reduce", 0
    )
    group = math.gcd(blocks, 4)
    grad_atom = pl.pallas_call(
        final_kernel,
        grid_spec=pltpu.PrefetchScalarGridSpec(
            num_scalar_prefetch=1,
            grid=(blocks // group,),
            in_specs=[
                whole(returned),
                pl.BlockSpec((group, 16, width), one),
                pl.BlockSpec((group, channels, width), one),
                pl.BlockSpec((group, filters * channels, width), one),
            ],
            out_specs=pl.BlockSpec((channels, filters * channels), lambda *_: (0, 0)),
            scratch_shapes=[pltpu.VMEM((blocks, channels, width), F32)],
        ),
        out_shape=jax.ShapeDtypeStruct((channels, filters * channels), F32),
        compiler_params=params,
        cost_estimate=cost(10e9),
        name="atom_grad",
    )(asked_ids, returned, where, message, sums)
    (grad_atom,) = reduce_all((grad_atom,), axes, "atom_reduce", 1)
    return (density.reshape(tiles, probes), grad_atom, grad_filter, grad_mix, grad_readout[0])


def solution(mesh):
    return jax.shard_map(
        body,
        mesh=mesh,
        in_specs=(
            P(("space", "tile"), None, None),
            P(("space", "tile"), None, None),
            P(("space", "tile")),
            P(("space", "tile"), None),
            P(("space", "tile"), None, None),
            P(("space", "tile"), None),
            P(("space", "tile"), None),
            P(),
            P(),
            P(),
            P(),
        ),
        out_specs=(P(("space", "tile"), None), P(), P(), P(), P()),
        check_vma=False,
    )
```

time: 210 us -> 203 us (0.967)
  waiting for transfers between devices: 52.8 us -> 0.02 us
  Pallas kernels: 114 us -> 149 us
  local copies, waits for them, and re-layouts: 13.9 us -> 27.4 us
  other arithmetic: 8.81 us -> 4.59 us
    pallas_call x1 -> x4, Pallas kernels: 37 us -> 108 us  [the longest x2 66.2 us: reduce_all(): pl.pallas_call(functools.partial(reduce_kernel, axes, len(grads)), in_spe...]
    all_to_all x2, waiting for transfers between devices: 28.8 us -> 0.01 us  [the longest x1 0.01 us: body(): lax.all_to_all(jnp.concatenate([flat_where, asked_row], axis=1), 'tile',...]
    all_to_all x1, waiting for transfers between devices: 23.9 us -> 0.01 us  [body(): lax.all_to_all(slot_grad.reshape(peers, cap, channels, width), 'tile', sp...]
    unnamed x22 -> x33, local copies, waits for them, and re-layouts: 7.31 us -> 23.7 us
    pallas_call x1, Pallas kernels: 31 us -> 15.7 us  [body(): pl.pallas_call(probe_kernel, grid_spec=pltpu.PrefetchScalarGridSpec(num_s...]
    pallas_call x1, Pallas kernels: 33.7 us -> 18.9 us  [body(): pl.pallas_call(atom_kernel, grid_spec=pltpu.PrefetchScalarGridSpec(num_sc...]
    pallas_call x1, Pallas kernels: 12.7 us -> 6.59 us  [body(): pl.pallas_call(final_kernel, grid_spec=pltpu.PrefetchScalarGridSpec(num_s...]
  transfers between devices with their start and end apart: 7 -> 7, of which waited for: 3 -> 0; matrix products, arithmetic and copies ran while one was open for 4% -> 4% of each run, Pallas kernels for 0% -> 40%
where the time goes in v2:
time: 203 us; the launch traced here: 201 us
  Pallas kernels  149 us (73%)
  local copies, waits for them, and re-layouts  27.4 us (13%)
  starting transfers between devices  19.6 us (10%)
  other arithmetic  4.59 us (2%)
    pallas_call x2, Pallas kernels, reduce_all(): pl.pallas_call(functools.partial(reduce_kernel, axes, len(grads)), in_spe...  66.2 us
    unnamed x33, local copies, waits for them, and re-layouts  23.7 us
    pallas_call x1, Pallas kernels, body(): pl.pallas_call(atom_radial_kernel, grid_spec=pltpu.PrefetchScalarGridSpec...  23 us
    pallas_call x1, Pallas kernels, body(): pl.pallas_call(atom_kernel, grid_spec=pltpu.PrefetchScalarGridSpec(num_sc...  18.9 us
    pallas_call x1, Pallas kernels, body(): pl.pallas_call(probe_radial_kernel, grid=(tiles, pieces), in_specs=[pl.Bl...  18.6 us
    pallas_call x1, Pallas kernels, body(): pl.pallas_call(probe_kernel, grid_spec=pltpu.PrefetchScalarGridSpec(num_s...  15.7 us
    pallas_call x1, Pallas kernels, body(): pl.pallas_call(final_kernel, grid_spec=pltpu.PrefetchScalarGridSpec(num_s...  6.59 us
    all_to_all x1, starting transfers between devices, body(): lax.all_to_all(jnp.concatenate([flat_where, asked_row], axis=1), 'tile',...  5.56 us
  transfers between devices with their start and end apart: 7, of which 0 were waited for; matrix products, arithmetic and copies ran while one was open for 4% of the time, Pallas kernels for 40%

profile of v2, /device:TPU:1, one launch (start us, length us, event | category | flops | bytes accessed | tf_op | source)
XLA Modules:
  0.0 201.5 jit_solution(18238885543351115891)
XLA Ops:
  0.6 0.7 compare_convert_fusion
  1.4 0.7 copy.29
  2.2 2.6 %collective-permute-start.2 = (bf16[16,16,128]{2,1,0:T(8,128)(2,1)S(1)}, bf16[16,16,128]{2,1,0:T(8,128)(2,1)S(1)}, u32[]{:S(2)}, u32[]{:S(2)}) collective-permute-start(bf16[16,16,128]{2,1,0:T(8,128)(2,1)S(1)} %pad_maximum_fusion.1.own_where_ref.where_ref), channel_id=1, source_target_pairs={{0,8},{8,16},{16,24},{24,0},{1,9},{9,17},{17,25},{25,1},{2,10},{10... | collective-permute-start | bytes 196616 | tf_op jit(solution)/shard_map/ppermute | solution.py:383
  5.4 0.7 multiply_add_fusion
  7.0 0.7 fusion.1
  7.7 5.6 %all-to-all-start = ((bf16[8,64,128]{2,1,0:T(8,128)(2,1)}), bf16[8,64,128]{2,1,0:T(8,128)(2,1)S(1)}, u32[]{:S(2)}, u32[]{:S(2)}) async-start(bf16[8,64,128]{2,1,0:T(8,128)(2,1)} %fusion.1), calls=%async_computation | async-start | bytes 262144 | tf_op jit(solution)/shard_map/all_to_all | solution.py:406
  13.8 1.3 reshape.202.target_ref
  15.6 0.7 add_select_fusion
  16.6 0.7 copy.32.where_ref
  17.5 23.0 %atom_radial.1.radial_ref = bf16[16,512,1024]{2,1,0:T(8,128)(2,1)S(1)} custom-call(s32[64]{0:T(128)S(1)} %multiply_add_fusion.1.rows_ref, bf16[48,16,128]{2,1,0:T(8,128)(2,1)S(1)} %pad_maximum_fusion.around_where_ref, bf16[16,16,128]{2,1,0:T(8,128)(2,1)S(1)} %pad_maximum_fusion.1.own_where_ref.where_ref), custom_call_target="tpu_custom_call" | custom-call | flops 20000000000 | bytes 1048576 | tf_op jit(solution)/shard_map/atom_radial/pallas_call | solution.py:414
  40.5 5.7 %copy-done.1 = bf16[16,512,1024]{2,1,0:T(8,128)(2,1)} copy-done((bf16[16,512,1024]{2,1,0:T(8,128)(2,1)}, bf16[16,512,1024]{2,1,0:T(8,128)(2,1)S(1)}, u32[]{:S(2)}) %copy-start.1) | copy-done | bytes 16777240
  46.3 0.7 reshape.207.asked_ref.ids_ref
  47.1 0.8 copy-done.11
  47.8 0.8 copy-done.12
  48.6 18.9 %atom_layer.1 = (bf16[32,128,128]{2,1,0:T(8,128)(2,1)}, bf16[16,1024,128]{2,1,0:T(8,128)(2,1)}, f32[16,128,128]{2,1,0:T(8,128)}) custom-call(s32[64]{0:T(128)} %copy-done.10, s32[64]{0:T(128)} %copy-done.9, s32[32]{0:T(128)} %reshape.207.asked_ref.ids_ref, bf16[16,128,128]{2,1,0:T(8,128)(2,1)} %copy-done.11, bf16[16,128,128]{2,1,0:T(8,128)(2,1)} %own_ref.1, ...), custom_call_target="tpu_custom_call" | custom-call | flops 10000000000 | bytes 1048576 | tf_op jit(solution)/shard_map/atom_layer/pallas_call | solution.py:429
  67.6 5.4 %all-to-all-start.1 = ((bf16[8,4,128,128]{3,2,1,0:T(8,128)(2,1)}), bf16[8,4,128,128]{3,2,1,0:T(8,128)(2,1)S(1)}, u32[]{:S(2)}, u32[]{:S(2)}) async-start(bf16[8,4,128,128]{3,2,1,0:T(8,128)(2,1)} %bitcast.16), calls=%async_computation.1 | async-start | bytes 2097152 | tf_op jit(solution)/shard_map/all_to_all | solution.py:463
  73.7 18.6 %probe_radial.1.radial_ref = bf16[2,1024,4096]{2,1,0:T(8,128)(2,1)S(1)} custom-call(f32[16,8,128]{2,1,0:T(8,128)S(1)} %pad_convert_fusion.source_ref, f32[2,3,512]{2,1,0:T(4,128)S(1)} %copy.32.where_ref), custom_call_target="tpu_custom_call" | custom-call | flops 20000000000 | bytes 1048576 | tf_op jit(solution)/shard_map/probe_radial/pallas_call | solution.py:472
  92.3 5.7 %copy-done.2 = bf16[2,1024,4096]{2,1,0:T(8,128)(2,1)} copy-done((bf16[2,1024,4096]{2,1,0:T(8,128)(2,1)}, bf16[2,1024,4096]{2,1,0:T(8,128)(2,1)S(1)}, u32[]{:S(2)}) %copy-start.2) | copy-done | bytes 16777240
  98.0 1.0 copy-done.7
  99.0 15.7 %probe_layer.1 = (f32[2,1,512]{2,1,0:T(1,128)}, f32[128,1024]{1,0:T(8,128)}, f32[128,128]{1,0:T(8,128)}, f32[8,128]{1,0:T(8,128)}, bf16[32,128,128]{2,1,0:T(8,128)(2,1)}) custom-call(s32[16]{0:T(128)} %multiply_add_fusion.2.slots_ref, bf16[32,128,128]{2,1,0:T(8,128)(2,1)} %bitcast.14, bf16[2,1024,4096]{2,1,0:T(8,128)(2,1)} %copy-done.2, ...), custom_call_target="tpu_custom_call" | custom-call | flops 10000000000 | bytes 1048576 | tf_op jit(solution)/shard_map/probe_layer/pallas_call | solution.py:488
  114.7 1.3 copy.36
  116.0 5.4 %all-to-all-start.2 = ((bf16[8,4,128,128]{3,2,1,0:T(8,128)(2,1)}), bf16[8,4,128,128]{3,2,1,0:T(8,128)(2,1)S(1)}, u32[]{:S(2)}, u32[]{:S(2)}) async-start(bf16[8,4,128,128]{3,2,1,0:T(8,128)(2,1)} %bitcast.17), calls=%async_computation.2 | async-start | bytes 2097152 | tf_op jit(solution)/shard_map/all_to_all | solution.py:530
  121.4 1.0 copy-done.3
  122.4 0.8 copy-done.5
  123.3 0.7 copy-done.6
  124.0 39.0 %probe_reduce.1 = (f32[128,1024]{1,0:T(8,128)S(1)}, f32[128,128]{1,0:T(8,128)S(1)}, f32[8,128]{1,0:T(8,128)S(1)}) custom-call(f32[128,1024]{1,0:T(8,128)S(1)} %copy-done.3, f32[128,128]{1,0:T(8,128)S(1)} %copy-done.5, f32[8,128]{1,0:T(8,128)S(1)} %copy-done.6), custom_call_target="tpu_custom_call" | custom-call | flops 20000000000 | bytes 1048576 | tf_op jit(solution)/shard_map/probe_reduce/pallas_call | solution.py:331
  163.5 1.0 copy-done.8
  164.4 6.6 %atom_grad.1.refs_0_ = f32[128,1024]{1,0:T(8,128)} custom-call(s32[32]{0:T(128)} %reshape.207.asked_ref.ids_ref, bf16[32,128,128]{2,1,0:T(8,128)(2,1)} %bitcast.15, bf16[16,16,128]{2,1,0:T(8,128)(2,1)} %copy-done, f32[16,128,128]{2,1,0:T(8,128)} %get-tuple-element.23.message_ref, bf16[16,1024,128]{2,1,0:T(8,128)(2,1)} %get-tuple-element.24.sums_ref), custom_call_target="tpu_custom_call" | custom-call | flops 10000000000 | bytes 1048576 | tf_op jit(solution)/shard_map/atom_grad/pallas_call | solution.py:539
  171.0 1.0 copy-done.4
  172.1 27.2 %atom_reduce.1 = f32[128,1024]{1,0:T(8,128)S(1)} custom-call(f32[128,1024]{1,0:T(8,128)S(1)} %copy-done.4), custom_call_target="tpu_custom_call" | custom-call | flops 20000000000 | bytes 1048576 | tf_op jit(solution)/shard_map/atom_reduce/pallas_call | solution.py:331
  199.3 0.8 copy.40
  200.1 0.8 copy.41
  (61 shorter events, 4.9 us)
Async XLA Ops:
  2.2 38.3 %copy-start = (bf16[16,16,128]{2,1,0:T(8,128)(2,1)}, bf16[16,16,128]{2,1,0:T(8,128)(2,1)S(1)}, u32[]{:S(2)}) copy-start(bf16[16,16,128]{2,1,0:T(8,128)(2,1)S(1)} %pad_maximum_fusion.1.own_where_ref.where_ref) | copy-start | bytes 196612
  2.2 15.2 %collective-permute-start.3 = (bf16[16,16,128]{2,1,0:T(8,128)(2,1)S(1)}, bf16[16,16,128]{2,1,0:T(8,128)(2,1)S(1)}, u32[]{:S(2)}, u32[]{:S(2)}) collective-permute-start(bf16[16,16,128]{2,1,0:T(8,128)(2,1)S(1)} %pad_maximum_fusion.1.own_where_ref.where_ref), channel_id=1, source_target_pairs={{8,0},{16,8},{24,16},{0,24},{9,1},{17,9},{25,17},{1,25},{10,2},{18... | collective-permute-start | bytes 196616 | tf_op jit(solution)/shard_map/ppermute | solution.py:383
  2.2 15.1 %collective-permute-start.2 = (bf16[16,16,128]{2,1,0:T(8,128)(2,1)S(1)}, bf16[16,16,128]{2,1,0:T(8,128)(2,1)S(1)}, u32[]{:S(2)}, u32[]{:S(2)}) collective-permute-start(bf16[16,16,128]{2,1,0:T(8,128)(2,1)S(1)} %pad_maximum_fusion.1.own_where_ref.where_ref), channel_id=1, source_target_pairs={{0,8},{8,16},{16,24},{24,0},{1,9},{9,17},{17,25},{25,1},{2,10},{10... | collective-permute-start | bytes 196616 | tf_op jit(solution)/shard_map/ppermute | solution.py:383
  4.9 42.1 %collective-permute-start = (bf16[16,128,128]{2,1,0:T(8,128)(2,1)}, bf16[16,128,128]{2,1,0:T(8,128)(2,1)S(1)}, u32[]{:S(2)}, u32[]{:S(2)}) collective-permute-start(bf16[16,128,128]{2,1,0:T(8,128)(2,1)} %own_ref.1), channel_id=1, source_target_pairs={{0,8},{8,16},{16,24},{24,0},{1,9},{9,17},{17,25},{25,1},{2,10},{10... | collective-permute-start | bytes 1572872 | tf_op jit(solution)/shard_map/ppermute | solution.py:380
  5.3 41.7 %collective-permute-start.1 = (bf16[16,128,128]{2,1,0:T(8,128)(2,1)}, bf16[16,128,128]{2,1,0:T(8,128)(2,1)S(1)}, u32[]{:S(2)}, u32[]{:S(2)}) collective-permute-start(bf16[16,128,128]{2,1,0:T(8,128)(2,1)} %own_ref.1), channel_id=1, source_target_pairs={{8,0},{16,8},{24,16},{0,24},{9,1},{17,9},{25,17},{1,25},{10,2},{18... | collective-permute-start | bytes 1572872 | tf_op jit(solution)/shard_map/ppermute | solution.py:381
  7.7 38.6 %all-to-all-start = ((bf16[8,64,128]{2,1,0:T(8,128)(2,1)}), bf16[8,64,128]{2,1,0:T(8,128)(2,1)S(1)}, u32[]{:S(2)}, u32[]{:S(2)}) async-start(bf16[8,64,128]{2,1,0:T(8,128)(2,1)} %fusion.1), calls=%async_computation | async-start | bytes 262144 | tf_op jit(solution)/shard_map/all_to_all | solution.py:406
  16.4 24.1 %copy-start.9 = (s32[64]{0:T(128)}, s32[64]{0:T(128)S(1)}, u32[]{:S(2)}) copy-start(s32[64]{0:T(128)S(1)} %reshape.198.sides_ref) | copy-start | bytes 772
  16.6 23.9 %copy-start.10 = (s32[64]{0:T(128)}, s32[64]{0:T(128)S(1)}, u32[]{:S(2)}) copy-start(s32[64]{0:T(128)S(1)} %reshape.197.rows_ref) | copy-start | bytes 772
  40.5 5.7 %copy-start.1 = (bf16[16,512,1024]{2,1,0:T(8,128)(2,1)}, bf16[16,512,1024]{2,1,0:T(8,128)(2,1)S(1)}, u32[]{:S(2)}) copy-start(bf16[16,512,1024]{2,1,0:T(8,128)(2,1)S(1)} %atom_radial.1.radial_ref) | copy-start | bytes 50331652
  47.0 0.8 copy-start.11
  47.8 0.8 copy-start.12
  67.6 30.4 %all-to-all-start.1 = ((bf16[8,4,128,128]{3,2,1,0:T(8,128)(2,1)}), bf16[8,4,128,128]{3,2,1,0:T(8,128)(2,1)S(1)}, u32[]{:S(2)}, u32[]{:S(2)}) async-start(bf16[8,4,128,128]{3,2,1,0:T(8,128)(2,1)} %bitcast.16), calls=%async_computation.1 | async-start | bytes 2097152 | tf_op jit(solution)/shard_map/all_to_all | solution.py:463
  92.3 5.7 %copy-start.2 = (bf16[2,1024,4096]{2,1,0:T(8,128)(2,1)}, bf16[2,1024,4096]{2,1,0:T(8,128)(2,1)S(1)}, u32[]{:S(2)}) copy-start(bf16[2,1024,4096]{2,1,0:T(8,128)(2,1)S(1)} %probe_radial.1.radial_ref) | copy-start | bytes 50331652
  98.0 1.0 copy-start.7
  116.0 47.5 %all-to-all-start.2 = ((bf16[8,4,128,128]{3,2,1,0:T(8,128)(2,1)}), bf16[8,4,128,128]{3,2,1,0:T(8,128)(2,1)S(1)}, u32[]{:S(2)}, u32[]{:S(2)}) async-start(bf16[8,4,128,128]{3,2,1,0:T(8,128)(2,1)} %bitcast.17), calls=%async_computation.2 | async-start | bytes 2097152 | tf_op jit(solution)/shard_map/all_to_all | solution.py:530
  121.4 1.0 copy-start.3
  122.4 0.8 copy-start.5
  123.3 0.7 copy-start.6
  163.5 1.0 copy-start.8
  171.0 1.0 copy-start.4

commit v3 on v2

--- a/solution.py
+++ b/solution.py
@@ -13,7 +13,7 @@
 SPREAD = 0.75
 LOG2E = 1.4426950408889634
 MESH = pl.DeviceIdType.MESH
-VMEM_LIMIT = 56 * 1024 * 1024
+VMEM_LIMIT = 60 * 1024 * 1024
 F32 = jnp.float32
 BF16 = jnp.bfloat16
 
@@ -43,19 +43,19 @@
     if keep is not None:
         centre = centre * keep
     ratio = 2.0 * step * LOG2E
-    up = jnp.exp2(shifted * ratio - step * step * LOG2E)
-    down = jnp.exp2(shifted * (-ratio) - step * step * LOG2E)
+    up = jnp.exp2(shifted * ratio)
+    down = jnp.exp2(shifted * (-ratio))
     values = [None] * filters
     values[middle] = centre
-    now = centre
-    for k in range(filters - 1 - middle):
-        now = now * (up if k == 0 else up * math.exp(-2.0 * k * step * step))
-        values[middle + k + 1] = now
-    now = centre
-    for k in range(middle):
-        now = now * (down if k == 0 else down * math.exp(-2.0 * k * step * step))
-        values[middle - k - 1] = now
+    for r in range(middle + 1, filters):
+        values[r] = values[r - 1] * up
+    for r in range(middle - 1, -1, -1):
+        values[r] = values[r + 1] * down
     return values
+
+
+def filter_weight(r, filters):
+    return math.exp(-(((r - filters // 2) * SPACING / SPREAD) ** 2))
 
 
 def dot(a, b):
@@ -111,9 +111,10 @@
             def _(ref=ref, row=row, part=part):
                 feats[part] = ref[row]
 
-    total = dot(feats[...], radial_ref[0]).astype(BF16)
+    total = dot(feats[...], radial_ref[0])
     for r in range(filters):
-        sums_ref[0, r * channels : (r + 1) * channels, :] = total[:, r * width : (r + 1) * width]
+        part = total[:, r * width : (r + 1) * width] * filter_weight(r, filters)
+        sums_ref[0, r * channels : (r + 1) * channels, :] = part.astype(BF16)
     message = dot(filter_ref[...], sums_ref[0])
     message_ref[0] = message
     keep = where_ref[0].astype(F32)[3:4, :]
@@ -177,9 +178,8 @@
     for k in range(reads):
         feats[:, k * width : (k + 1) * width] = replies_ref[slots_ref[tile * reads + k]]
     for r in range(filters):
-        summed[r * channels : (r + 1) * channels, :] = dot(
-            feats[...], radial_ref[0, :, r * probes : (r + 1) * probes]
-        ).astype(BF16)
+        part = dot(feats[...], radial_ref[0, :, r * probes : (r + 1) * probes])
+        summed[r * channels : (r + 1) * channels, :] = (part * filter_weight(r, filters)).astype(BF16)
     hidden = dot(filter_ref[...], summed[...])
     gate = jax.nn.sigmoid(hidden)
     squashed = (hidden * gate).astype(BF16)
@@ -199,9 +199,10 @@
     grad_squashed = dot(mix_ref[...].T, grad_mixed)
     grad_hidden = (grad_squashed * (gate * (1.0 + hidden * (1.0 - gate)))).astype(BF16)
     grad_filter_ref[...] += dot_nt(grad_hidden, summed[...])
-    grad_sums = dot(grad_hidden.T, filter_ref[...]).astype(BF16)
+    grad_sums = dot(grad_hidden.T, filter_ref[...])
     for r in range(filters):
-        turned[r * probes : (r + 1) * probes, :] = grad_sums[:, r * channels : (r + 1) * channels]
+        part = grad_sums[:, r * channels : (r + 1) * channels] * filter_weight(r, filters)
+        turned[r * probes : (r + 1) * probes, :] = part.astype(BF16)
     for k in range(reads):
         slot = slots_ref[tile * reads + k]
         back = dot(radial_ref[0, k * width : (k + 1) * width, :], turned[...])
@@ -248,19 +249,15 @@
 def reduce_kernel(axes, count, *refs):
     ins, outs = refs[:count], refs[count : 2 * count]
     total, sending, landing, gathered, send_sems, recv_sems = refs[2 * count :]
-    lanes = total.shape[1]
-    rows = total.shape[0]
-    partners = []
+    rows, lanes = total.shape
+    peers = []
     for axis, size in axes:
         here = lax.axis_index(axis)
-        bit = 1
-        while bit < size:
-            side = (here // bit) % 2
-            partners.append((axis, here + bit * (1 - 2 * side), side))
-            bit *= 2
+        peers.append((here, [(here + d) % size for d in range(1, size)]))
     barrier = pltpu.get_barrier_semaphore()
-    for axis, other, _ in partners:
-        pl.semaphore_signal(barrier, inc=1, device_id={axis: other}, device_id_type=MESH)
+    for (axis, _), (_, others) in zip(axes, peers):
+        for other in others:
+            pl.semaphore_signal(barrier, inc=1, device_id={axis: other}, device_id_type=MESH)
     pieces = []
     low = 0
     for index, ref in enumerate(ins):
@@ -271,53 +268,59 @@
             low += height
     if low < rows:
         total[low:, :] = jnp.zeros((rows - low, lanes), F32)
-    pl.semaphore_wait(barrier, len(partners))
-    start = 0
-    size = rows
-    place = 0
-    copies = []
-    ranges = []
-    for n, (axis, other, side) in enumerate(partners):
-        size //= 2
-        keep = pl.multiple_of(start + side * size, 16)
-        give = pl.multiple_of(start + (1 - side) * size, 16)
-        sending[place : place + size, :] = total[pl.ds(give, size), :].astype(BF16)
+    pl.semaphore_wait(barrier, sum(size - 1 for _, size in axes))
+    sent = []
+
+    def send(source, target, axis, other):
+        n = len(sent)
         copy = pltpu.make_async_remote_copy(
-            src_ref=sending.at[pl.ds(place, size)],
-            dst_ref=landing.at[pl.ds(place, size)],
+            src_ref=source,
+            dst_ref=target,
             send_sem=send_sems.at[n],
             recv_sem=recv_sems.at[n],
             device_id={axis: other},
             device_id_type=MESH,
         )
         copy.start()
-        copy.wait_recv()
-        total[pl.ds(keep, size), :] += landing[place : place + size, :].astype(F32)
-        copies.append(copy)
-        ranges.append((keep, size))
-        place += size
-        start = keep
-    keep, size = ranges[-1]
-    gathered[pl.ds(keep, size), :] = total[pl.ds(keep, size), :].astype(BF16)
-    for n in range(len(partners) - 1, -1, -1):
-        axis, other, _ = partners[n]
-        keep, size = ranges[n]
-        copy = pltpu.make_async_remote_copy(
-            src_ref=gathered.at[pl.ds(keep, size)],
-            dst_ref=gathered.at[pl.ds(keep, size)],
-            send_sem=send_sems.at[len(partners) + n],
-            recv_sem=recv_sems.at[len(partners) + n],
-            device_id={axis: other},
-            device_id_type=MESH,
-        )
-        copy.start()
-        copy.wait_recv()
-        copies.append(copy)
+        sent.append(copy)
+        return copy
+
+    start, extent, place, bases = 0, rows, 0, []
+    for (axis, size), (here, others) in zip(axes, peers):
+        sending[place : place + extent, :] = total[pl.ds(start, extent), :].astype(BF16)
+        part = extent // size
+        copies = []
+        for d, other in enumerate(others):
+            copies.append(
+                send(
+                    sending.at[pl.ds(pl.multiple_of(place + other * part, 16), part)],
+                    landing.at[pl.ds(place + d * part, part)],
+                    axis,
+                    other,
+                )
+            )
+        bases.append((start, extent))
+        start = pl.multiple_of(start + here * part, 16)
+        for d, copy in enumerate(copies):
+            copy.wait_recv()
+            total[pl.ds(start, part), :] += landing[
+                place + d * part : place + (d + 1) * part, :
+            ].astype(F32)
+        place += extent
+        extent = part
+    gathered[pl.ds(start, extent), :] = total[pl.ds(start, extent), :].astype(BF16)
+    for n in range(len(axes) - 1, -1, -1):
+        axis = axes[n][0]
+        mine = gathered.at[pl.ds(start, extent)]
+        copies = [send(mine, mine, axis, other) for other in peers[n][1]]
+        for copy in copies:
+            copy.wait_recv()
+        start, extent = bases[n]
     for index, left, low, height in pieces:
         padded = -(-height // 16) * 16
         part = gathered[low : low + padded, :].astype(F32)[:height]
         outs[index][:, left : left + lanes] = part
-    for copy in copies:
+    for copy in sent:
         copy.wait_send()
 
 
@@ -326,7 +329,8 @@
     lanes = grads[0].shape[0]
     real = sum(-(-g.size // (16 * lanes)) * 16 for g in grads)
     rows = -(-real // (16 * devices)) * 16 * devices
-    steps = (devices - 1).bit_length()
+    steps = sum(size - 1 for _, size in axes)
+    spare = rows + rows // axes[0][1]
     vmem = pl.BlockSpec(memory_space=pltpu.VMEM)
     return pl.pallas_call(
         functools.partial(reduce_kernel, axes, len(grads)),
@@ -335,14 +339,14 @@
         out_shape=[jax.ShapeDtypeStruct(g.shape, F32) for g in grads],
         scratch_shapes=[
             pltpu.VMEM((rows, lanes), F32),
-            pltpu.VMEM((rows, lanes), BF16),
-            pltpu.VMEM((rows, lanes), BF16),
+            pltpu.VMEM((spare, lanes), BF16),
+            pltpu.VMEM((spare, lanes), BF16),
             pltpu.VMEM((rows, lanes), BF16),
             pltpu.SemaphoreType.DMA((2 * steps,)),
             pltpu.SemaphoreType.DMA((2 * steps,)),
         ],
         compiler_params=pltpu.CompilerParams(
-            vmem_limit_bytes=16 * 1024 * 1024, collective_id=collective_id, has_side_effects=True
+            vmem_limit_bytes=VMEM_LIMIT, collective_id=collective_id, has_side_effects=True
         ),
         cost_estimate=cost(20e9),
         name=name,
@@ -370,7 +374,7 @@
     space_count = lax.axis_size("space")
     here = lax.axis_index("space")
     params = pltpu.CompilerParams(vmem_limit_bytes=VMEM_LIMIT)
-    small = pltpu.CompilerParams(vmem_limit_bytes=16 * 1024 * 1024)
+    small = params
     mask = (jnp.arange(width)[None, :] < atom_counts[:, None]).astype(BF16)
     where = jnp.concatenate(
         [atom_pos, mask[:, None, :], jnp.zeros((blocks, 12, width), BF16)], axis=1
@@ -454,7 +458,7 @@
             jax.ShapeDtypeStruct((blocks, filters * channels, width), BF16),
             jax.ShapeDtypeStruct((blocks, channels, width), F32),
         ],
-        compiler_params=params,
+        compiler_params=small,
         cost_estimate=cost(10e9),
         name="atom_layer",
     )(near_rows, sides, asked_ids, low_feat, atom_feat, high_feat, atom_radial, where, atom_filter)

time: 203 us -> 191 us (0.941)
  local copies, waits for them, and re-layouts: 27.4 us -> 14.6 us
  Pallas kernels: 149 us -> 145 us
  waiting for transfers between devices: 0.02 us -> 3.2 us
    unnamed x33 -> x25, local copies, waits for them, and re-layouts: 23.7 us -> 10.3 us
    pallas_call x2, Pallas kernels: 66.2 us -> 59.9 us  [reduce_all(): pl.pallas_call(functools.partial(reduce_kernel, axes, len(grads)), in_spe...]
    all_to_all x1, waiting for transfers between devices: 0.01 us -> 3.18 us  [body(): lax.all_to_all(sent.reshape(peers, cap, channels, width), 'tile', split_a...]
  transfers between devices with their start and end apart: 7 -> 7, of which waited for: 0 -> 1; matrix products, arithmetic and copies ran while one was open for 4% -> 6% of each run, Pallas kernels for 40% -> 44%
where the time goes in v3:
time: 191 us; the launch traced here: 190 us
  Pallas kernels  145 us (76%)
  starting transfers between devices  19.6 us (10%)
  local copies, waits for them, and re-layouts  14.6 us (8%)
  other arithmetic  6.46 us (3%)
  waiting for transfers between devices  3.2 us (2%)
    pallas_call x2, Pallas kernels, reduce_all(): pl.pallas_call(functools.partial(reduce_kernel, axes, len(grads)), in_spe...  59.9 us
    pallas_call x1, Pallas kernels, body(): pl.pallas_call(atom_radial_kernel, grid_spec=pltpu.PrefetchScalarGridSpec...  24.2 us
    pallas_call x1, Pallas kernels, body(): pl.pallas_call(probe_radial_kernel, grid=(tiles, pieces), in_specs=[pl.Bl...  19.7 us
    pallas_call x1, Pallas kernels, body(): pl.pallas_call(atom_kernel, grid_spec=pltpu.PrefetchScalarGridSpec(num_sc...  19 us
    pallas_call x1, Pallas kernels, body(): pl.pallas_call(probe_kernel, grid_spec=pltpu.PrefetchScalarGridSpec(num_s...  15.7 us
    unnamed x25, local copies, waits for them, and re-layouts  10.3 us
    pallas_call x1, Pallas kernels, body(): pl.pallas_call(final_kernel, grid_spec=pltpu.PrefetchScalarGridSpec(num_s...  6.59 us
    all_to_all x1, starting transfers between devices, body(): lax.all_to_all(jnp.concatenate([flat_where, asked_row], axis=1), 'tile',...  5.56 us
  transfers between devices with their start and end apart: 7, of which 1 were waited for; matrix products, arithmetic and copies ran while one was open for 6% of the time, Pallas kernels for 44%

profile of v3, /device:TPU:1, one launch (start us, length us, event | category | flops | bytes accessed | tf_op | source)
XLA Modules:
  0.0 189.7 jit_solution(10115381015508470733)
XLA Ops:
  0.6 0.7 compare_convert_fusion
  1.4 0.7 copy.29
  2.2 2.6 %collective-permute-start.2 = (bf16[16,16,128]{2,1,0:T(8,128)(2,1)S(1)}, bf16[16,16,128]{2,1,0:T(8,128)(2,1)S(1)}, u32[]{:S(2)}, u32[]{:S(2)}) collective-permute-start(bf16[16,16,128]{2,1,0:T(8,128)(2,1)S(1)} %pad_maximum_fusion.1.own_where_ref.where_ref), channel_id=1, source_target_pairs={{0,8},{8,16},{16,24},{24,0},{1,9},{9,17},{17,25},{25,1},{2,10},{10... | collective-permute-start | bytes 196616 | tf_op jit(solution)/shard_map/ppermute | solution.py:387
  5.4 0.7 multiply_add_fusion
  7.0 0.7 fusion.1
  7.7 5.6 %all-to-all-start = ((bf16[8,64,128]{2,1,0:T(8,128)(2,1)}), bf16[8,64,128]{2,1,0:T(8,128)(2,1)S(1)}, u32[]{:S(2)}, u32[]{:S(2)}) async-start(bf16[8,64,128]{2,1,0:T(8,128)(2,1)} %fusion.1), calls=%async_computation | async-start | bytes 262144 | tf_op jit(solution)/shard_map/all_to_all | solution.py:410
  13.8 1.3 reshape.202.target_ref
  15.6 0.7 add_select_fusion
  16.6 1.3 copy.32.where_ref
  18.0 0.6 multiply_add_fusion.1.rows_ref
  18.5 0.7 pad_maximum_fusion.around_where_ref
  19.3 24.2 %atom_radial.1.radial_ref = bf16[16,512,1024]{2,1,0:T(8,128)(2,1)} custom-call(s32[64]{0:T(128)} %multiply_add_fusion.1.rows_ref, bf16[48,16,128]{2,1,0:T(8,128)(2,1)} %pad_maximum_fusion.around_where_ref, bf16[16,16,128]{2,1,0:T(8,128)(2,1)} %copy-done.3), custom_call_target="tpu_custom_call" | custom-call | flops 20000000000 | bytes 1048576 | tf_op jit(solution)/shard_map/atom_radial/pallas_call | solution.py:418
  44.2 0.8 copy-done.7
  45.0 0.8 copy-done.8
  45.8 19.0 %atom_layer.1 = (bf16[32,128,128]{2,1,0:T(8,128)(2,1)}, bf16[16,1024,128]{2,1,0:T(8,128)(2,1)}, f32[16,128,128]{2,1,0:T(8,128)}) custom-call(s32[64]{0:T(128)} %copy-done.6, s32[64]{0:T(128)} %copy-done.5, s32[32]{0:T(128)} %reshape.207.asked_ref.ids_ref, bf16[16,128,128]{2,1,0:T(8,128)(2,1)} %copy-done.7, bf16[16,128,128]{2,1,0:T(8,128)(2,1)} %own_ref.1, ...), custom_call_target="tpu_custom_call" | custom-call | flops 10000000000 | bytes 1048576 | tf_op jit(solution)/shard_map/atom_layer/pallas_call | solution.py:433
  64.7 5.4 %all-to-all-start.1 = ((bf16[8,4,128,128]{3,2,1,0:T(8,128)(2,1)}), bf16[8,4,128,128]{3,2,1,0:T(8,128)(2,1)S(1)}, u32[]{:S(2)}, u32[]{:S(2)}) async-start(bf16[8,4,128,128]{3,2,1,0:T(8,128)(2,1)} %bitcast.16), calls=%async_computation.1 | async-start | bytes 2097152 | tf_op jit(solution)/shard_map/all_to_all | solution.py:467
  70.2 0.6 gather_fusion
  70.9 0.6 pad_convert_fusion.source_ref
  71.5 19.7 %probe_radial.1.radial_ref = bf16[2,1024,4096]{2,1,0:T(8,128)(2,1)} custom-call(f32[16,8,128]{2,1,0:T(8,128)} %pad_convert_fusion.source_ref, f32[2,3,512]{2,1,0:T(4,128)} %copy.32.where_ref), custom_call_target="tpu_custom_call" | custom-call | flops 20000000000 | bytes 1048576 | tf_op jit(solution)/shard_map/probe_radial/pallas_call | solution.py:476
  91.2 3.2 %all-to-all-done.1 = bf16[8,4,128,128]{3,2,1,0:T(8,128)(2,1)S(1)} async-done(((bf16[8,4,128,128]{3,2,1,0:T(8,128)(2,1)}), bf16[8,4,128,128]{3,2,1,0:T(8,128)(2,1)S(1)}, u32[]{:S(2)}, u32[]{:S(2)}) %all-to-all-start.1) | async-done | bytes 1048608 | tf_op jit(solution)/shard_map/all_to_all | solution.py:467
  94.4 1.0 copy-done
  95.4 15.7 %probe_layer.1 = (f32[2,1,512]{2,1,0:T(1,128)}, f32[128,1024]{1,0:T(8,128)}, f32[128,128]{1,0:T(8,128)}, f32[8,128]{1,0:T(8,128)}, bf16[32,128,128]{2,1,0:T(8,128)(2,1)}) custom-call(s32[16]{0:T(128)} %multiply_add_fusion.2.slots_ref, bf16[32,128,128]{2,1,0:T(8,128)(2,1)} %bitcast.14, bf16[2,1024,4096]{2,1,0:T(8,128)(2,1)} %probe_radial.1.radial_ref, ...), custom_call_target="tpu_custom_call" | custom-call | flops 10000000000 | bytes 1048576 | tf_op jit(solution)/shard_map/probe_layer/pallas_call | solution.py:492
  111.0 1.3 copy.36
  112.3 5.4 %all-to-all-start.2 = ((bf16[8,4,128,128]{3,2,1,0:T(8,128)(2,1)}), bf16[8,4,128,128]{3,2,1,0:T(8,128)(2,1)S(1)}, u32[]{:S(2)}, u32[]{:S(2)}) async-start(bf16[8,4,128,128]{3,2,1,0:T(8,128)(2,1)} %bitcast.17), calls=%async_computation.2 | async-start | bytes 2097152 | tf_op jit(solution)/shard_map/all_to_all | solution.py:534
  117.7 39.2 %probe_reduce.1 = (f32[128,1024]{1,0:T(8,128)}, f32[128,128]{1,0:T(8,128)}, f32[8,128]{1,0:T(8,128)}) custom-call(f32[128,1024]{1,0:T(8,128)} %get-tuple-element.25.refs_0_, f32[128,128]{1,0:T(8,128)} %get-tuple-element.26.refs_1_, f32[8,128]{1,0:T(8,128)} %get-tuple-element.27.refs_2_), custom_call_target="tpu_custom_call" | custom-call | flops 20000000000 | bytes 1048576 | tf_op jit(solution)/shard_map/probe_reduce/pallas_call | solution.py:335
  156.9 1.2 slice_bitcast_fusion
  158.1 1.0 copy-done.1
  159.0 6.6 %atom_grad.1.refs_0_ = f32[128,1024]{1,0:T(8,128)} custom-call(s32[32]{0:T(128)} %reshape.207.asked_ref.ids_ref, bf16[32,128,128]{2,1,0:T(8,128)(2,1)} %bitcast.15, bf16[16,16,128]{2,1,0:T(8,128)(2,1)} %copy-done.3, f32[16,128,128]{2,1,0:T(8,128)} %get-tuple-element.23.message_ref, bf16[16,1024,128]{2,1,0:T(8,128)(2,1)} %get-tuple-element.24.sums_ref), custom_call_target="tpu_custom_call" | custom-call | flops 10000000000 | bytes 1048576 | tf_op jit(solution)/shard_map/atom_grad/pallas_call | solution.py:543
  165.6 20.7 %atom_reduce.1 = f32[128,1024]{1,0:T(8,128)} custom-call(f32[128,1024]{1,0:T(8,128)} %atom_grad.1.refs_0_), custom_call_target="tpu_custom_call" | custom-call | flops 20000000000 | bytes 1048576 | tf_op jit(solution)/shard_map/atom_reduce/pallas_call | solution.py:335
  186.4 1.9 copy.40
  188.2 0.8 copy.41
  189.0 0.6 copy.42
  (53 shorter events, 3.7 us)
Async XLA Ops:
  2.2 17.1 %copy-start.3 = (bf16[16,16,128]{2,1,0:T(8,128)(2,1)}, bf16[16,16,128]{2,1,0:T(8,128)(2,1)S(1)}, u32[]{:S(2)}) copy-start(bf16[16,16,128]{2,1,0:T(8,128)(2,1)S(1)} %pad_maximum_fusion.1.own_where_ref.where_ref) | copy-start | bytes 196612
  2.2 16.4 %collective-permute-start.3 = (bf16[16,16,128]{2,1,0:T(8,128)(2,1)S(1)}, bf16[16,16,128]{2,1,0:T(8,128)(2,1)S(1)}, u32[]{:S(2)}, u32[]{:S(2)}) collective-permute-start(bf16[16,16,128]{2,1,0:T(8,128)(2,1)S(1)} %pad_maximum_fusion.1.own_where_ref.where_ref), channel_id=1, source_target_pairs={{8,0},{16,8},{24,16},{0,24},{9,1},{17,9},{25,17},{1,25},{10,2},{18... | collective-permute-start | bytes 196616 | tf_op jit(solution)/shard_map/ppermute | solution.py:387
  2.2 16.3 %collective-permute-start.2 = (bf16[16,16,128]{2,1,0:T(8,128)(2,1)S(1)}, bf16[16,16,128]{2,1,0:T(8,128)(2,1)S(1)}, u32[]{:S(2)}, u32[]{:S(2)}) collective-permute-start(bf16[16,16,128]{2,1,0:T(8,128)(2,1)S(1)} %pad_maximum_fusion.1.own_where_ref.where_ref), channel_id=1, source_target_pairs={{0,8},{8,16},{16,24},{24,0},{1,9},{9,17},{17,25},{25,1},{2,10},{10... | collective-permute-start | bytes 196616 | tf_op jit(solution)/shard_map/ppermute | solution.py:387
  4.9 39.3 %collective-permute-start = (bf16[16,128,128]{2,1,0:T(8,128)(2,1)}, bf16[16,128,128]{2,1,0:T(8,128)(2,1)S(1)}, u32[]{:S(2)}, u32[]{:S(2)}) collective-permute-start(bf16[16,128,128]{2,1,0:T(8,128)(2,1)} %own_ref.1), channel_id=1, source_target_pairs={{0,8},{8,16},{16,24},{24,0},{1,9},{9,17},{17,25},{25,1},{2,10},{10... | collective-permute-start | bytes 1572872 | tf_op jit(solution)/shard_map/ppermute | solution.py:384
  5.3 38.9 %collective-permute-start.1 = (bf16[16,128,128]{2,1,0:T(8,128)(2,1)}, bf16[16,128,128]{2,1,0:T(8,128)(2,1)S(1)}, u32[]{:S(2)}, u32[]{:S(2)}) collective-permute-start(bf16[16,128,128]{2,1,0:T(8,128)(2,1)} %own_ref.1), channel_id=1, source_target_pairs={{8,0},{16,8},{24,16},{0,24},{9,1},{17,9},{25,17},{1,25},{10,2},{18... | collective-permute-start | bytes 1572872 | tf_op jit(solution)/shard_map/ppermute | solution.py:385
  7.7 35.9 %all-to-all-start = ((bf16[8,64,128]{2,1,0:T(8,128)(2,1)}), bf16[8,64,128]{2,1,0:T(8,128)(2,1)S(1)}, u32[]{:S(2)}, u32[]{:S(2)}) async-start(bf16[8,64,128]{2,1,0:T(8,128)(2,1)} %fusion.1), calls=%async_computation | async-start | bytes 262144 | tf_op jit(solution)/shard_map/all_to_all | solution.py:410
  16.4 27.1 %copy-start.5 = (s32[64]{0:T(128)}, s32[64]{0:T(128)S(1)}, u32[]{:S(2)}) copy-start(s32[64]{0:T(128)S(1)} %reshape.198.sides_ref) | copy-start | bytes 772
  16.6 26.9 %copy-start.6 = (s32[64]{0:T(128)}, s32[64]{0:T(128)S(1)}, u32[]{:S(2)}) copy-start(s32[64]{0:T(128)S(1)} %reshape.197.rows_ref) | copy-start | bytes 772
  44.2 0.8 copy-start.7
  45.0 0.8 copy-start.8
  64.7 29.6 %all-to-all-start.1 = ((bf16[8,4,128,128]{3,2,1,0:T(8,128)(2,1)}), bf16[8,4,128,128]{3,2,1,0:T(8,128)(2,1)S(1)}, u32[]{:S(2)}, u32[]{:S(2)}) async-start(bf16[8,4,128,128]{3,2,1,0:T(8,128)(2,1)} %bitcast.16), calls=%async_computation.1 | async-start | bytes 2097152 | tf_op jit(solution)/shard_map/all_to_all | solution.py:467
  94.4 1.0 copy-start
  112.3 45.8 %all-to-all-start.2 = ((bf16[8,4,128,128]{3,2,1,0:T(8,128)(2,1)}), bf16[8,4,128,128]{3,2,1,0:T(8,128)(2,1)S(1)}, u32[]{:S(2)}, u32[]{:S(2)}) async-start(bf16[8,4,128,128]{3,2,1,0:T(8,128)(2,1)} %bitcast.17), calls=%async_computation.2 | async-start | bytes 2097152 | tf_op jit(solution)/shard_map/all_to_all | solution.py:534
  158.1 1.0 copy-start.1
  165.6 22.6 %copy-start.2 = (f32[128,1024]{1,0:T(8,128)S(1)}, f32[128,1024]{1,0:T(8,128)}, u32[]{:S(2)}) copy-start(f32[128,1024]{1,0:T(8,128)} %get-tuple-element.45) | copy-start | bytes 1572868
  165.6 23.4 %copy-start.4 = (f32[128,128]{1,0:T(8,128)S(1)}, f32[128,128]{1,0:T(8,128)}, u32[]{:S(2)}) copy-start(f32[128,128]{1,0:T(8,128)} %get-tuple-element.46) | copy-start | bytes 196612

commit v4 on v3

--- a/solution.py
+++ b/solution.py
@@ -32,9 +32,9 @@
     distance = square * lax.rsqrt(square)
     half = (math.pi / (2.0 * CUTOFF)) ** 2
     terms = [math.sqrt(factor) * (-half) ** k / math.factorial(2 * k) for k in range(7)]
-    wave = terms[6] * square + terms[5]
-    for term in terms[4::-1]:
-        wave = wave * square + term
+    second = square * square
+    wave = (terms[0] + terms[1] * square) + (terms[2] + terms[3] * square) * second
+    wave = wave + ((terms[4] + terms[5] * square) + terms[6] * second) * (second * second)
     envelope = jnp.where(square < CUTOFF * CUTOFF, wave * wave, 0.0)
     middle = filters // 2
     shifted = distance * (1.0 / SPREAD) - middle * (SPACING / SPREAD)
@@ -43,19 +43,17 @@
     if keep is not None:
         centre = centre * keep
     ratio = 2.0 * step * LOG2E
-    up = jnp.exp2(shifted * ratio)
-    down = jnp.exp2(shifted * (-ratio))
+    up = jnp.exp2(shifted * ratio - step * step * LOG2E)
+    down = jnp.exp2(shifted * (-ratio) - step * step * LOG2E)
     values = [None] * filters
     values[middle] = centre
     for r in range(middle + 1, filters):
-        values[r] = values[r - 1] * up
+        k = r - middle - 1
+        values[r] = values[r - 1] * (up if k == 0 else up * math.exp(-2.0 * k * step * step))
     for r in range(middle - 1, -1, -1):
-        values[r] = values[r + 1] * down
+        k = middle - 1 - r
+        values[r] = values[r + 1] * (down if k == 0 else down * math.exp(-2.0 * k * step * step))
     return values
-
-
-def filter_weight(r, filters):
-    return math.exp(-(((r - filters // 2) * SPACING / SPREAD) ** 2))
 
 
 def dot(a, b):
@@ -87,7 +85,7 @@
             radial_ref[0, pl.ds(start, chunk), r * width : (r + 1) * width] = value.astype(BF16)
         return carry
 
-    lax.fori_loop(0, nbrs * width // chunk, fill, 0, unroll=2)
+    lax.fori_loop(0, nbrs * width // chunk, fill, 0, unroll=4)
 
 
 def atom_kernel(
@@ -113,7 +111,7 @@
 
     total = dot(feats[...], radial_ref[0])
     for r in range(filters):
-        part = total[:, r * width : (r + 1) * width] * filter_weight(r, filters)
+        part = total[:, r * width : (r + 1) * width]
         sums_ref[0, r * channels : (r + 1) * channels, :] = part.astype(BF16)
     message = dot(filter_ref[...], sums_ref[0])
     message_ref[0] = message
@@ -152,7 +150,7 @@
                 radial_ref[0, pl.ds(start, chunk), low : low + span] = value.astype(BF16)
         return carry
 
-    lax.fori_loop(0, reads * width // chunk, fill, 0)
+    lax.fori_loop(0, reads * width // chunk, fill, 0, unroll=2)
 
 
 def probe_kernel(
@@ -179,7 +177,7 @@
         feats[:, k * width : (k + 1) * width] = replies_ref[slots_ref[tile * reads + k]]
     for r in range(filters):
         part = dot(feats[...], radial_ref[0, :, r * probes : (r + 1) * probes])
-        summed[r * channels : (r + 1) * channels, :] = (part * filter_weight(r, filters)).astype(BF16)
+        summed[r * channels : (r + 1) * channels, :] = (part).astype(BF16)
     hidden = dot(filter_ref[...], summed[...])
     gate = jax.nn.sigmoid(hidden)
     squashed = (hidden * gate).astype(BF16)
@@ -201,7 +199,7 @@
     grad_filter_ref[...] += dot_nt(grad_hidden, summed[...])
     grad_sums = dot(grad_hidden.T, filter_ref[...])
     for r in range(filters):
-        part = grad_sums[:, r * channels : (r + 1) * channels] * filter_weight(r, filters)
+        part = grad_sums[:, r * channels : (r + 1) * channels]
         turned[r * probes : (r + 1) * probes, :] = part.astype(BF16)
     for k in range(reads):
         slot = slots_ref[tile * reads + k]
@@ -536,9 +534,6 @@
         split_axis=0, concat_axis=0, tiled=True,
     ).reshape(slots, channels, width)
     axes = (("space", space_count), ("tile", peers))
-    grad_filter, grad_mix, grad_readout = reduce_all(
-        (grad_filter, grad_mix, grad_readout), axes, "probe_reduce", 0
-    )
     group = math.gcd(blocks, 4)
     grad_atom = pl.pallas_call(
         final_kernel,
@@ -559,7 +554,9 @@
         cost_estimate=cost(10e9),
         name="atom_grad",
     )(asked_ids, returned, where, message, sums)
-    (grad_atom,) = reduce_all((grad_atom,), axes, "atom_reduce", 1)
+    grad_atom, grad_filter, grad_mix, grad_readout = reduce_all(
+        (grad_atom, grad_filter, grad_mix, grad_readout), axes, "grad_reduce", 0
+    )
     return (density.reshape(tiles, probes), grad_atom, grad_filter, grad_mix, grad_readout[0])
 
 

time: 191 us -> 183 us (0.958)
  Pallas kernels: 145 us -> 108 us
  waiting for transfers between devices: 3.2 us -> 30.7 us
    pallas_call x2 -> x1, Pallas kernels: 59.9 us -> 31.4 us  [reduce_all(): pl.pallas_call(functools.partial(reduce_kernel, axes, len(grads)), in_spe...]
    all_to_all x1, waiting for transfers between devices: 0.01 us -> 23.8 us  [body(): lax.all_to_all(slot_grad.reshape(peers, cap, channels, width), 'tile', sp...]
    pallas_call x1, Pallas kernels: 24.2 us -> 19.2 us  [body(): pl.pallas_call(atom_radial_kernel, grid_spec=pltpu.PrefetchScalarGridSpec...]
    pallas_call x1, Pallas kernels: 19.7 us -> 16 us  [body(): pl.pallas_call(probe_radial_kernel, grid=(tiles, pieces), in_specs=[pl.Bl...]
    all_to_all x1, waiting for transfers between devices: 3.18 us -> 6.88 us  [body(): lax.all_to_all(sent.reshape(peers, cap, channels, width), 'tile', split_a...]
    unnamed x25 -> x21, local copies, waits for them, and re-layouts: 10.3 us -> 12.2 us
  transfers between devices with their start and end apart: 7 -> 7, of which waited for: 1 -> 2; matrix products, arithmetic and copies ran while one was open for 6% -> 6% of each run, Pallas kernels for 44% -> 19%
where the time goes in v4:
time: 183 us; the launch traced here: 182 us
  Pallas kernels  108 us (59%)
  waiting for transfers between devices  30.7 us (17%)
  starting transfers between devices  19.6 us (11%)
  local copies, waits for them, and re-layouts  16.5 us (9%)
  other arithmetic  6.37 us (3%)
    pallas_call x1, Pallas kernels, reduce_all(): pl.pallas_call(functools.partial(reduce_kernel, axes, len(grads)), in_spe...  31.4 us
    all_to_all x1, waiting for transfers between devices, body(): lax.all_to_all(slot_grad.reshape(peers, cap, channels, width), 'tile', sp...  23.8 us
    pallas_call x1, Pallas kernels, body(): pl.pallas_call(atom_radial_kernel, grid_spec=pltpu.PrefetchScalarGridSpec...  19.2 us
    pallas_call x1, Pallas kernels, body(): pl.pallas_call(atom_kernel, grid_spec=pltpu.PrefetchScalarGridSpec(num_sc...  18.9 us
    pallas_call x1, Pallas kernels, body(): pl.pallas_call(probe_radial_kernel, grid=(tiles, pieces), in_specs=[pl.Bl...  16 us
    pallas_call x1, Pallas kernels, body(): pl.pallas_call(probe_kernel, grid_spec=pltpu.PrefetchScalarGridSpec(num_s...  15.6 us
    unnamed x21, local copies, waits for them, and re-layouts  12.2 us
    all_to_all x1, waiting for transfers between devices, body(): lax.all_to_all(sent.reshape(peers, cap, channels, width), 'tile', split_a...  6.88 us
  transfers between devices with their start and end apart: 7, of which 2 were waited for; matrix products, arithmetic and copies ran while one was open for 6% of the time, Pallas kernels for 19%

profile of v4, /device:TPU:1, one launch (start us, length us, event | category | flops | bytes accessed | tf_op | source)
XLA Modules:
  0.0 181.6 jit_solution(5383096800940284629)
XLA Ops:
  0.6 0.7 compare_convert_fusion
  1.4 0.7 copy.29
  2.2 2.6 %collective-permute-start.2 = (bf16[16,16,128]{2,1,0:T(8,128)(2,1)S(1)}, bf16[16,16,128]{2,1,0:T(8,128)(2,1)S(1)}, u32[]{:S(2)}, u32[]{:S(2)}) collective-permute-start(bf16[16,16,128]{2,1,0:T(8,128)(2,1)S(1)} %pad_maximum_fusion.1.own_where_ref.where_ref), channel_id=1, source_target_pairs={{0,8},{8,16},{16,24},{24,0},{1,9},{9,17},{17,25},{25,1},{2,10},{10... | collective-permute-start | bytes 196616 | tf_op jit(solution)/shard_map/ppermute | solution.py:385
  5.4 0.7 multiply_add_fusion
  7.0 0.7 fusion.1
  7.7 5.6 %all-to-all-start = ((bf16[8,64,128]{2,1,0:T(8,128)(2,1)}), bf16[8,64,128]{2,1,0:T(8,128)(2,1)S(1)}, u32[]{:S(2)}, u32[]{:S(2)}) async-start(bf16[8,64,128]{2,1,0:T(8,128)(2,1)} %fusion.1), calls=%async_computation | async-start | bytes 262144 | tf_op jit(solution)/shard_map/all_to_all | solution.py:408
  13.8 1.3 reshape.202.target_ref
  15.6 0.7 add_select_fusion
  16.6 1.3 copy.32.where_ref
  18.5 0.7 pad_maximum_fusion.around_where_ref
  19.2 19.2 %atom_radial.1.radial_ref = bf16[16,512,1024]{2,1,0:T(8,128)(2,1)} custom-call(s32[64]{0:T(128)} %multiply_add_fusion.1.rows_ref, bf16[48,16,128]{2,1,0:T(8,128)(2,1)} %pad_maximum_fusion.around_where_ref, bf16[16,16,128]{2,1,0:T(8,128)(2,1)} %copy-done.2), custom_call_target="tpu_custom_call" | custom-call | flops 20000000000 | bytes 1048576 | tf_op jit(solution)/shard_map/atom_radial/pallas_call | solution.py:416
  38.4 0.6 reshape.207.asked_ref.ids_ref
  39.1 0.8 copy-done.5
  39.9 0.8 copy-done.6
  40.6 18.9 %atom_layer.1 = (bf16[32,128,128]{2,1,0:T(8,128)(2,1)}, bf16[16,1024,128]{2,1,0:T(8,128)(2,1)}, f32[16,128,128]{2,1,0:T(8,128)}) custom-call(s32[64]{0:T(128)} %copy-done.4, s32[64]{0:T(128)} %copy-done.3, s32[32]{0:T(128)} %reshape.207.asked_ref.ids_ref, bf16[16,128,128]{2,1,0:T(8,128)(2,1)} %copy-done.5, bf16[16,128,128]{2,1,0:T(8,128)(2,1)} %own_ref.1, ...), custom_call_target="tpu_custom_call" | custom-call | flops 10000000000 | bytes 1048576 | tf_op jit(solution)/shard_map/atom_layer/pallas_call | solution.py:431
  59.6 5.4 %all-to-all-start.1 = ((bf16[8,4,128,128]{3,2,1,0:T(8,128)(2,1)}), bf16[8,4,128,128]{3,2,1,0:T(8,128)(2,1)S(1)}, u32[]{:S(2)}, u32[]{:S(2)}) async-start(bf16[8,4,128,128]{3,2,1,0:T(8,128)(2,1)} %bitcast.15), calls=%async_computation.1 | async-start | bytes 2097152 | tf_op jit(solution)/shard_map/all_to_all | solution.py:465
  65.0 0.6 gather_fusion
  65.7 0.6 pad_convert_fusion.source_ref
  66.3 16.0 %probe_radial.1.radial_ref = bf16[2,1024,4096]{2,1,0:T(8,128)(2,1)} custom-call(f32[16,8,128]{2,1,0:T(8,128)} %pad_convert_fusion.source_ref, f32[2,3,512]{2,1,0:T(4,128)} %copy.32.where_ref), custom_call_target="tpu_custom_call" | custom-call | flops 20000000000 | bytes 1048576 | tf_op jit(solution)/shard_map/probe_radial/pallas_call | solution.py:474
  82.3 6.9 %all-to-all-done.1 = bf16[8,4,128,128]{3,2,1,0:T(8,128)(2,1)S(1)} async-done(((bf16[8,4,128,128]{3,2,1,0:T(8,128)(2,1)}), bf16[8,4,128,128]{3,2,1,0:T(8,128)(2,1)S(1)}, u32[]{:S(2)}, u32[]{:S(2)}) %all-to-all-start.1) | async-done | bytes 1048608 | tf_op jit(solution)/shard_map/all_to_all | solution.py:465
  89.2 1.0 copy-done
  90.2 15.6 %probe_layer.1 = (f32[2,1,512]{2,1,0:T(1,128)}, f32[128,1024]{1,0:T(8,128)}, f32[128,128]{1,0:T(8,128)}, f32[8,128]{1,0:T(8,128)}, bf16[32,128,128]{2,1,0:T(8,128)(2,1)}) custom-call(s32[16]{0:T(128)} %multiply_add_fusion.2.slots_ref, bf16[32,128,128]{2,1,0:T(8,128)(2,1)} %bitcast.14, bf16[2,1024,4096]{2,1,0:T(8,128)(2,1)} %probe_radial.1.radial_ref, ...), custom_call_target="tpu_custom_call" | custom-call | flops 10000000000 | bytes 1048576 | tf_op jit(solution)/shard_map/probe_layer/pallas_call | solution.py:490
  105.8 5.4 %all-to-all-start.2 = ((bf16[8,4,128,128]{3,2,1,0:T(8,128)(2,1)}), bf16[8,4,128,128]{3,2,1,0:T(8,128)(2,1)S(1)}, u32[]{:S(2)}, u32[]{:S(2)}) async-start(bf16[8,4,128,128]{3,2,1,0:T(8,128)(2,1)} %bitcast.17), calls=%async_computation.2 | async-start | bytes 2097152 | tf_op jit(solution)/shard_map/all_to_all | solution.py:532
  111.2 1.3 copy.36
  112.5 23.8 %all-to-all-done.2 = bf16[8,4,128,128]{3,2,1,0:T(8,128)(2,1)S(1)} async-done(((bf16[8,4,128,128]{3,2,1,0:T(8,128)(2,1)}), bf16[8,4,128,128]{3,2,1,0:T(8,128)(2,1)S(1)}, u32[]{:S(2)}, u32[]{:S(2)}) %all-to-all-start.2) | async-done | bytes 1048608 | tf_op jit(solution)/shard_map/all_to_all | solution.py:532
  136.3 1.0 copy-done.1
  137.2 6.6 %atom_grad.1.refs_0_ = f32[128,1024]{1,0:T(8,128)} custom-call(s32[32]{0:T(128)} %reshape.207.asked_ref.ids_ref, bf16[32,128,128]{2,1,0:T(8,128)(2,1)} %bitcast.16, bf16[16,16,128]{2,1,0:T(8,128)(2,1)} %copy-done.2, f32[16,128,128]{2,1,0:T(8,128)} %get-tuple-element.24.message_ref, bf16[16,1024,128]{2,1,0:T(8,128)(2,1)} %get-tuple-element.25.sums_ref), custom_call_target="tpu_custom_call" | custom-call | flops 10000000000 | bytes 1048576 | tf_op jit(solution)/shard_map/atom_grad/pallas_call | solution.py:538
  143.8 31.4 %grad_reduce.1 = (f32[128,1024]{1,0:T(8,128)}, f32[128,1024]{1,0:T(8,128)}, f32[128,128]{1,0:T(8,128)}, f32[8,128]{1,0:T(8,128)}) custom-call(f32[128,1024]{1,0:T(8,128)} %atom_grad.1.refs_0_, f32[128,1024]{1,0:T(8,128)} %get-tuple-element.26.refs_1_, f32[128,128]{1,0:T(8,128)} %get-tuple-element.27.refs_2_, f32[8,128]{1,0:T(8,128)} %get-tuple-element.28.refs_3_), custom_call_target="tpu_custom_call" | custom-call | flops 20000000000 | bytes 1048576 | tf_op jit(solution)/shard_map/grad_reduce/pallas_call | solution.py:333
  175.2 1.2 slice_bitcast_fusion
  176.4 1.9 %copy.40 = f32[128,1024]{1,0:T(8,128)} copy(f32[128,1024]{1,0:T(8,128)} %get-tuple-element.46) | data formatting | bytes 1048576
  178.2 1.9 %copy.41 = f32[128,1024]{1,0:T(8,128)} copy(f32[128,1024]{1,0:T(8,128)} %get-tuple-element.47) | data formatting | bytes 1048576
  180.1 1.5 copy.42
  (48 shorter events, 3.6 us)
Async XLA Ops:
  2.2 17.0 %copy-start.2 = (bf16[16,16,128]{2,1,0:T(8,128)(2,1)}, bf16[16,16,128]{2,1,0:T(8,128)(2,1)S(1)}, u32[]{:S(2)}) copy-start(bf16[16,16,128]{2,1,0:T(8,128)(2,1)S(1)} %pad_maximum_fusion.1.own_where_ref.where_ref) | copy-start | bytes 196612
  2.2 16.3 %collective-permute-start.3 = (bf16[16,16,128]{2,1,0:T(8,128)(2,1)S(1)}, bf16[16,16,128]{2,1,0:T(8,128)(2,1)S(1)}, u32[]{:S(2)}, u32[]{:S(2)}) collective-permute-start(bf16[16,16,128]{2,1,0:T(8,128)(2,1)S(1)} %pad_maximum_fusion.1.own_where_ref.where_ref), channel_id=1, source_target_pairs={{8,0},{16,8},{24,16},{0,24},{9,1},{17,9},{25,17},{1,25},{10,2},{18... | collective-permute-start | bytes 196616 | tf_op jit(solution)/shard_map/ppermute | solution.py:385
  2.2 16.2 %collective-permute-start.2 = (bf16[16,16,128]{2,1,0:T(8,128)(2,1)S(1)}, bf16[16,16,128]{2,1,0:T(8,128)(2,1)S(1)}, u32[]{:S(2)}, u32[]{:S(2)}) collective-permute-start(bf16[16,16,128]{2,1,0:T(8,128)(2,1)S(1)} %pad_maximum_fusion.1.own_where_ref.where_ref), channel_id=1, source_target_pairs={{0,8},{8,16},{16,24},{24,0},{1,9},{9,17},{17,25},{25,1},{2,10},{10... | collective-permute-start | bytes 196616 | tf_op jit(solution)/shard_map/ppermute | solution.py:385
  4.9 34.2 %collective-permute-start = (bf16[16,128,128]{2,1,0:T(8,128)(2,1)}, bf16[16,128,128]{2,1,0:T(8,128)(2,1)S(1)}, u32[]{:S(2)}, u32[]{:S(2)}) collective-permute-start(bf16[16,128,128]{2,1,0:T(8,128)(2,1)} %own_ref.1), channel_id=1, source_target_pairs={{0,8},{8,16},{16,24},{24,0},{1,9},{9,17},{17,25},{25,1},{2,10},{10... | collective-permute-start | bytes 1572872 | tf_op jit(solution)/shard_map/ppermute | solution.py:382
  5.3 33.7 %collective-permute-start.1 = (bf16[16,128,128]{2,1,0:T(8,128)(2,1)}, bf16[16,128,128]{2,1,0:T(8,128)(2,1)S(1)}, u32[]{:S(2)}, u32[]{:S(2)}) collective-permute-start(bf16[16,128,128]{2,1,0:T(8,128)(2,1)} %own_ref.1), channel_id=1, source_target_pairs={{8,0},{16,8},{24,16},{0,24},{9,1},{17,9},{25,17},{1,25},{10,2},{18... | collective-permute-start | bytes 1572872 | tf_op jit(solution)/shard_map/ppermute | solution.py:383
  7.7 30.7 %all-to-all-start = ((bf16[8,64,128]{2,1,0:T(8,128)(2,1)}), bf16[8,64,128]{2,1,0:T(8,128)(2,1)S(1)}, u32[]{:S(2)}, u32[]{:S(2)}) async-start(bf16[8,64,128]{2,1,0:T(8,128)(2,1)} %fusion.1), calls=%async_computation | async-start | bytes 262144 | tf_op jit(solution)/shard_map/all_to_all | solution.py:408
  16.4 21.9 %copy-start.3 = (s32[64]{0:T(128)}, s32[64]{0:T(128)S(1)}, u32[]{:S(2)}) copy-start(s32[64]{0:T(128)S(1)} %reshape.198.sides_ref) | copy-start | bytes 772
  16.6 21.8 %copy-start.4 = (s32[64]{0:T(128)}, s32[64]{0:T(128)S(1)}, u32[]{:S(2)}) copy-start(s32[64]{0:T(128)S(1)} %reshape.197.rows_ref) | copy-start | bytes 772
  39.1 0.8 copy-start.5
  39.9 0.8 copy-start.6
  59.6 29.6 %all-to-all-start.1 = ((bf16[8,4,128,128]{3,2,1,0:T(8,128)(2,1)}), bf16[8,4,128,128]{3,2,1,0:T(8,128)(2,1)S(1)}, u32[]{:S(2)}, u32[]{:S(2)}) async-start(bf16[8,4,128,128]{3,2,1,0:T(8,128)(2,1)} %bitcast.15), calls=%async_computation.1 | async-start | bytes 2097152 | tf_op jit(solution)/shard_map/all_to_all | solution.py:465
  89.2 1.0 copy-start
  105.8 30.4 %all-to-all-start.2 = ((bf16[8,4,128,128]{3,2,1,0:T(8,128)(2,1)}), bf16[8,4,128,128]{3,2,1,0:T(8,128)(2,1)S(1)}, u32[]{:S(2)}, u32[]{:S(2)}) async-start(bf16[8,4,128,128]{3,2,1,0:T(8,128)(2,1)} %bitcast.17), calls=%async_computation.2 | async-start | bytes 2097152 | tf_op jit(solution)/shard_map/all_to_all | solution.py:532
  136.3 1.0 copy-start.1

commit v5 on v4

--- a/solution.py
+++ b/solution.py
@@ -85,7 +85,7 @@
             radial_ref[0, pl.ds(start, chunk), r * width : (r + 1) * width] = value.astype(BF16)
         return carry
 
-    lax.fori_loop(0, nbrs * width // chunk, fill, 0, unroll=4)
+    lax.fori_loop(0, nbrs * width // chunk, fill, 0, unroll=8)
 
 
 def atom_kernel(
@@ -150,7 +150,7 @@
                 radial_ref[0, pl.ds(start, chunk), low : low + span] = value.astype(BF16)
         return carry
 
-    lax.fori_loop(0, reads * width // chunk, fill, 0, unroll=2)
+    lax.fori_loop(0, reads * width // chunk, fill, 0, unroll=4)
 
 
 def probe_kernel(

time: 183 us -> 181 us (0.989)
  Pallas kernels: 108 us -> 103 us
  waiting for transfers between devices: 30.7 us -> 33 us
    all_to_all x1, waiting for transfers between devices: 6.88 us -> 9.26 us  [body(): lax.all_to_all(sent.reshape(peers, cap, channels, width), 'tile', split_a...]
    pallas_call x1, Pallas kernels: 16 us -> 13.6 us  [body(): pl.pallas_call(probe_radial_kernel, grid=(tiles, pieces), in_specs=[pl.Bl...]
    pallas_call x1, Pallas kernels: 19.2 us -> 17.3 us  [body(): pl.pallas_call(atom_radial_kernel, grid_spec=pltpu.PrefetchScalarGridSpec...]
  transfers between devices with their start and end apart: 7 -> 7, of which waited for: 2 -> 2; matrix products, arithmetic and copies ran while one was open for 6% -> 6% of each run, Pallas kernels for 19% -> 17%
where the time goes in v5:
time: 181 us; the launch traced here: 180 us
  Pallas kernels  103 us (57%)
  waiting for transfers between devices  33 us (18%)
  starting transfers between devices  19.6 us (11%)
  local copies, waits for them, and re-layouts  16.5 us (9%)
  other arithmetic  6.37 us (4%)
    pallas_call x1, Pallas kernels, reduce_all(): pl.pallas_call(functools.partial(reduce_kernel, axes, len(grads)), in_spe...  31.4 us
    all_to_all x1, waiting for transfers between devices, body(): lax.all_to_all(slot_grad.reshape(peers, cap, channels, width), 'tile', sp...  23.8 us
    pallas_call x1, Pallas kernels, body(): pl.pallas_call(atom_kernel, grid_spec=pltpu.PrefetchScalarGridSpec(num_sc...  18.9 us
    pallas_call x1, Pallas kernels, body(): pl.pallas_call(atom_radial_kernel, grid_spec=pltpu.PrefetchScalarGridSpec...  17.3 us
    pallas_call x1, Pallas kernels, body(): pl.pallas_call(probe_kernel, grid_spec=pltpu.PrefetchScalarGridSpec(num_s...  15.6 us
    pallas_call x1, Pallas kernels, body(): pl.pallas_call(probe_radial_kernel, grid=(tiles, pieces), in_specs=[pl.Bl...  13.6 us
    unnamed x21, local copies, waits for them, and re-layouts  12.2 us
    all_to_all x1, waiting for transfers between devices, body(): lax.all_to_all(sent.reshape(peers, cap, channels, width), 'tile', split_a...  9.26 us
  transfers between devices with their start and end apart: 7, of which 2 were waited for; matrix products, arithmetic and copies ran while one was open for 6% of the time, Pallas kernels for 17%

profile of v5, /device:TPU:1, one launch (start us, length us, event | category | flops | bytes accessed | tf_op | source)
XLA Modules:
  0.0 179.7 jit_solution(540168491850662858)
XLA Ops:
  0.6 0.7 compare_convert_fusion
  1.4 0.7 copy.29
  2.2 2.6 %collective-permute-start.2 = (bf16[16,16,128]{2,1,0:T(8,128)(2,1)S(1)}, bf16[16,16,128]{2,1,0:T(8,128)(2,1)S(1)}, u32[]{:S(2)}, u32[]{:S(2)}) collective-permute-start(bf16[16,16,128]{2,1,0:T(8,128)(2,1)S(1)} %pad_maximum_fusion.1.own_where_ref.where_ref), channel_id=1, source_target_pairs={{0,8},{8,16},{16,24},{24,0},{1,9},{9,17},{17,25},{25,1},{2,10},{10... | collective-permute-start | bytes 196616 | tf_op jit(solution)/shard_map/ppermute | solution.py:385
  5.4 0.7 multiply_add_fusion
  7.0 0.7 fusion.1
  7.7 5.6 %all-to-all-start = ((bf16[8,64,128]{2,1,0:T(8,128)(2,1)}), bf16[8,64,128]{2,1,0:T(8,128)(2,1)S(1)}, u32[]{:S(2)}, u32[]{:S(2)}) async-start(bf16[8,64,128]{2,1,0:T(8,128)(2,1)} %fusion.1), calls=%async_computation | async-start | bytes 262144 | tf_op jit(solution)/shard_map/all_to_all | solution.py:408
  13.8 1.3 reshape.202.target_ref
  15.6 0.7 add_select_fusion
  16.6 1.3 copy.32.where_ref
  18.5 0.7 pad_maximum_fusion.around_where_ref
  19.2 17.3 %atom_radial.1.radial_ref = bf16[16,512,1024]{2,1,0:T(8,128)(2,1)} custom-call(s32[64]{0:T(128)} %multiply_add_fusion.1.rows_ref, bf16[48,16,128]{2,1,0:T(8,128)(2,1)} %pad_maximum_fusion.around_where_ref, bf16[16,16,128]{2,1,0:T(8,128)(2,1)} %copy-done.2), custom_call_target="tpu_custom_call" | custom-call | flops 20000000000 | bytes 1048576 | tf_op jit(solution)/shard_map/atom_radial/pallas_call | solution.py:416
  36.5 0.6 reshape.207.asked_ref.ids_ref
  37.2 0.8 copy-done.5
  38.0 0.8 copy-done.6
  38.8 18.9 %atom_layer.1 = (bf16[32,128,128]{2,1,0:T(8,128)(2,1)}, bf16[16,1024,128]{2,1,0:T(8,128)(2,1)}, f32[16,128,128]{2,1,0:T(8,128)}) custom-call(s32[64]{0:T(128)} %copy-done.4, s32[64]{0:T(128)} %copy-done.3, s32[32]{0:T(128)} %reshape.207.asked_ref.ids_ref, bf16[16,128,128]{2,1,0:T(8,128)(2,1)} %copy-done.5, bf16[16,128,128]{2,1,0:T(8,128)(2,1)} %own_ref.1, ...), custom_call_target="tpu_custom_call" | custom-call | flops 10000000000 | bytes 1048576 | tf_op jit(solution)/shard_map/atom_layer/pallas_call | solution.py:431
  57.7 5.4 %all-to-all-start.1 = ((bf16[8,4,128,128]{3,2,1,0:T(8,128)(2,1)}), bf16[8,4,128,128]{3,2,1,0:T(8,128)(2,1)S(1)}, u32[]{:S(2)}, u32[]{:S(2)}) async-start(bf16[8,4,128,128]{3,2,1,0:T(8,128)(2,1)} %bitcast.15), calls=%async_computation.1 | async-start | bytes 2097152 | tf_op jit(solution)/shard_map/all_to_all | solution.py:465
  63.1 0.6 gather_fusion
  63.8 0.6 pad_convert_fusion.source_ref
  64.4 13.6 %probe_radial.1.radial_ref = bf16[2,1024,4096]{2,1,0:T(8,128)(2,1)} custom-call(f32[16,8,128]{2,1,0:T(8,128)} %pad_convert_fusion.source_ref, f32[2,3,512]{2,1,0:T(4,128)} %copy.32.where_ref), custom_call_target="tpu_custom_call" | custom-call | flops 20000000000 | bytes 1048576 | tf_op jit(solution)/shard_map/probe_radial/pallas_call | solution.py:474
  78.0 9.3 %all-to-all-done.1 = bf16[8,4,128,128]{3,2,1,0:T(8,128)(2,1)S(1)} async-done(((bf16[8,4,128,128]{3,2,1,0:T(8,128)(2,1)}), bf16[8,4,128,128]{3,2,1,0:T(8,128)(2,1)S(1)}, u32[]{:S(2)}, u32[]{:S(2)}) %all-to-all-start.1) | async-done | bytes 1048608 | tf_op jit(solution)/shard_map/all_to_all | solution.py:465
  87.3 1.0 copy-done
  88.3 15.6 %probe_layer.1 = (f32[2,1,512]{2,1,0:T(1,128)}, f32[128,1024]{1,0:T(8,128)}, f32[128,128]{1,0:T(8,128)}, f32[8,128]{1,0:T(8,128)}, bf16[32,128,128]{2,1,0:T(8,128)(2,1)}) custom-call(s32[16]{0:T(128)} %multiply_add_fusion.2.slots_ref, bf16[32,128,128]{2,1,0:T(8,128)(2,1)} %bitcast.14, bf16[2,1024,4096]{2,1,0:T(8,128)(2,1)} %probe_radial.1.radial_ref, ...), custom_call_target="tpu_custom_call" | custom-call | flops 10000000000 | bytes 1048576 | tf_op jit(solution)/shard_map/probe_layer/pallas_call | solution.py:490
  104.0 5.4 %all-to-all-start.2 = ((bf16[8,4,128,128]{3,2,1,0:T(8,128)(2,1)}), bf16[8,4,128,128]{3,2,1,0:T(8,128)(2,1)S(1)}, u32[]{:S(2)}, u32[]{:S(2)}) async-start(bf16[8,4,128,128]{3,2,1,0:T(8,128)(2,1)} %bitcast.17), calls=%async_computation.2 | async-start | bytes 2097152 | tf_op jit(solution)/shard_map/all_to_all | solution.py:532
  109.3 1.3 copy.36
  110.6 23.8 %all-to-all-done.2 = bf16[8,4,128,128]{3,2,1,0:T(8,128)(2,1)S(1)} async-done(((bf16[8,4,128,128]{3,2,1,0:T(8,128)(2,1)}), bf16[8,4,128,128]{3,2,1,0:T(8,128)(2,1)S(1)}, u32[]{:S(2)}, u32[]{:S(2)}) %all-to-all-start.2) | async-done | bytes 1048608 | tf_op jit(solution)/shard_map/all_to_all | solution.py:532
  134.4 1.0 copy-done.1
  135.3 6.6 %atom_grad.1.refs_0_ = f32[128,1024]{1,0:T(8,128)} custom-call(s32[32]{0:T(128)} %reshape.207.asked_ref.ids_ref, bf16[32,128,128]{2,1,0:T(8,128)(2,1)} %bitcast.16, bf16[16,16,128]{2,1,0:T(8,128)(2,1)} %copy-done.2, f32[16,128,128]{2,1,0:T(8,128)} %get-tuple-element.24.message_ref, bf16[16,1024,128]{2,1,0:T(8,128)(2,1)} %get-tuple-element.25.sums_ref), custom_call_target="tpu_custom_call" | custom-call | flops 10000000000 | bytes 1048576 | tf_op jit(solution)/shard_map/atom_grad/pallas_call | solution.py:538
  141.9 31.4 %grad_reduce.1 = (f32[128,1024]{1,0:T(8,128)}, f32[128,1024]{1,0:T(8,128)}, f32[128,128]{1,0:T(8,128)}, f32[8,128]{1,0:T(8,128)}) custom-call(f32[128,1024]{1,0:T(8,128)} %atom_grad.1.refs_0_, f32[128,1024]{1,0:T(8,128)} %get-tuple-element.26.refs_1_, f32[128,128]{1,0:T(8,128)} %get-tuple-element.27.refs_2_, f32[8,128]{1,0:T(8,128)} %get-tuple-element.28.refs_3_), custom_call_target="tpu_custom_call" | custom-call | flops 20000000000 | bytes 1048576 | tf_op jit(solution)/shard_map/grad_reduce/pallas_call | solution.py:333
  173.3 1.2 slice_bitcast_fusion
  174.5 1.9 %copy.40 = f32[128,1024]{1,0:T(8,128)} copy(f32[128,1024]{1,0:T(8,128)} %get-tuple-element.46) | data formatting | bytes 1048576
  176.4 1.9 %copy.41 = f32[128,1024]{1,0:T(8,128)} copy(f32[128,1024]{1,0:T(8,128)} %get-tuple-element.47) | data formatting | bytes 1048576
  178.3 1.5 copy.42
  (48 shorter events, 3.6 us)
Async XLA Ops:
  2.2 17.0 %copy-start.2 = (bf16[16,16,128]{2,1,0:T(8,128)(2,1)}, bf16[16,16,128]{2,1,0:T(8,128)(2,1)S(1)}, u32[]{:S(2)}) copy-start(bf16[16,16,128]{2,1,0:T(8,128)(2,1)S(1)} %pad_maximum_fusion.1.own_where_ref.where_ref) | copy-start | bytes 196612
  2.2 16.3 %collective-permute-start.3 = (bf16[16,16,128]{2,1,0:T(8,128)(2,1)S(1)}, bf16[16,16,128]{2,1,0:T(8,128)(2,1)S(1)}, u32[]{:S(2)}, u32[]{:S(2)}) collective-permute-start(bf16[16,16,128]{2,1,0:T(8,128)(2,1)S(1)} %pad_maximum_fusion.1.own_where_ref.where_ref), channel_id=1, source_target_pairs={{8,0},{16,8},{24,16},{0,24},{9,1},{17,9},{25,17},{1,25},{10,2},{18... | collective-permute-start | bytes 196616 | tf_op jit(solution)/shard_map/ppermute | solution.py:385
  2.2 16.2 %collective-permute-start.2 = (bf16[16,16,128]{2,1,0:T(8,128)(2,1)S(1)}, bf16[16,16,128]{2,1,0:T(8,128)(2,1)S(1)}, u32[]{:S(2)}, u32[]{:S(2)}) collective-permute-start(bf16[16,16,128]{2,1,0:T(8,128)(2,1)S(1)} %pad_maximum_fusion.1.own_where_ref.where_ref), channel_id=1, source_target_pairs={{0,8},{8,16},{16,24},{24,0},{1,9},{9,17},{17,25},{25,1},{2,10},{10... | collective-permute-start | bytes 196616 | tf_op jit(solution)/shard_map/ppermute | solution.py:385
  4.9 32.3 %collective-permute-start = (bf16[16,128,128]{2,1,0:T(8,128)(2,1)}, bf16[16,128,128]{2,1,0:T(8,128)(2,1)S(1)}, u32[]{:S(2)}, u32[]{:S(2)}) collective-permute-start(bf16[16,128,128]{2,1,0:T(8,128)(2,1)} %own_ref.1), channel_id=1, source_target_pairs={{0,8},{8,16},{16,24},{24,0},{1,9},{9,17},{17,25},{25,1},{2,10},{10... | collective-permute-start | bytes 1572872 | tf_op jit(solution)/shard_map/ppermute | solution.py:382
  5.3 31.9 %collective-permute-start.1 = (bf16[16,128,128]{2,1,0:T(8,128)(2,1)}, bf16[16,128,128]{2,1,0:T(8,128)(2,1)S(1)}, u32[]{:S(2)}, u32[]{:S(2)}) collective-permute-start(bf16[16,128,128]{2,1,0:T(8,128)(2,1)} %own_ref.1), channel_id=1, source_target_pairs={{8,0},{16,8},{24,16},{0,24},{9,1},{17,9},{25,17},{1,25},{10,2},{18... | collective-permute-start | bytes 1572872 | tf_op jit(solution)/shard_map/ppermute | solution.py:383
  7.7 28.8 %all-to-all-start = ((bf16[8,64,128]{2,1,0:T(8,128)(2,1)}), bf16[8,64,128]{2,1,0:T(8,128)(2,1)S(1)}, u32[]{:S(2)}, u32[]{:S(2)}) async-start(bf16[8,64,128]{2,1,0:T(8,128)(2,1)} %fusion.1), calls=%async_computation | async-start | bytes 262144 | tf_op jit(solution)/shard_map/all_to_all | solution.py:408
  16.4 20.1 %copy-start.3 = (s32[64]{0:T(128)}, s32[64]{0:T(128)S(1)}, u32[]{:S(2)}) copy-start(s32[64]{0:T(128)S(1)} %reshape.198.sides_ref) | copy-start | bytes 772
  16.6 19.9 %copy-start.4 = (s32[64]{0:T(128)}, s32[64]{0:T(128)S(1)}, u32[]{:S(2)}) copy-start(s32[64]{0:T(128)S(1)} %reshape.197.rows_ref) | copy-start | bytes 772
  37.2 0.8 copy-start.5
  38.0 0.8 copy-start.6
  57.7 29.6 %all-to-all-start.1 = ((bf16[8,4,128,128]{3,2,1,0:T(8,128)(2,1)}), bf16[8,4,128,128]{3,2,1,0:T(8,128)(2,1)S(1)}, u32[]{:S(2)}, u32[]{:S(2)}) async-start(bf16[8,4,128,128]{3,2,1,0:T(8,128)(2,1)} %bitcast.15), calls=%async_computation.1 | async-start | bytes 2097152 | tf_op jit(solution)/shard_map/all_to_all | solution.py:465
  87.3 1.0 copy-start
  104.0 30.4 %all-to-all-start.2 = ((bf16[8,4,128,128]{3,2,1,0:T(8,128)(2,1)}), bf16[8,4,128,128]{3,2,1,0:T(8,128)(2,1)S(1)}, u32[]{:S(2)}, u32[]{:S(2)}) async-start(bf16[8,4,128,128]{3,2,1,0:T(8,128)(2,1)} %bitcast.17), calls=%async_computation.2 | async-start | bytes 2097152 | tf_op jit(solution)/shard_map/all_to_all | solution.py:532
  134.4 1.0 copy-start.1
